TPU v7x, 32 devices: a whole 2x2x4 slice. The times are simulated.
32 devices in a mesh: mem: 4 (over y, x), lat: 4 (over z), win: 2 (over core).
Axes of the slice: x: 2, y: 2, z: 4, core: 2. Of those that a mesh axis runs over, the one named last changes fastest.
Arguments:
- ensemble: float32 [8, 8, 32, 512], P('mem', None, 'lat'), may hold values from -6 to 6
- weights: float32 [2, 8, 32, 512], P('win', 'mem', 'lat'), may hold values from -6 to 6
- diffusivity: float32 [8, 32, 512], P(None, 'lat', 'mem'), may hold values from 0.05 to 0.4
- coupling: float32 [8, 8], replicated, may hold values from -0.5 to 0.5
- tl_steps: int32 [2], P('win'), may hold values from 1 to 6
- obs_cell: int32 [16384], P(('mem', 'lat')), may hold values from 0 to 8191
- obs_window: int32 [16384], P(('mem', 'lat')), may hold values from 0 to 1
- obs_value: float32 [16384], P(('mem', 'lat')), may hold values from -6 to 6
- obs_weight: float32 [16384], P(('mem', 'lat')), may hold values from 1 to 8
- error_weight: float32 [8], replicated, may hold values from 0.5 to 4
Outputs:
- control: float32 [2, 8, 32, 512], P('win', 'mem', 'lat')
- increment: float32 [2, 8, 32, 512], P('win', None, 'lat', 'mem')
Inputs may be any that keep to these rules, and one draw needn't show every extreme that they name: `tl_steps`: how many of the 6 tangent steps the subwindow takes. `obs_cell`: index of the observed cell in the block of 8 x 8 x 128 cells that the observation's device holds (mem index, lat index), flattened as variable, row, longitude.
All inputs are finite; a program needn't handle non-finite values.
Results may differ from a plain program's by a relative error of at most 0.00015.
Values sent between devices are 32-bit elements; how exact they have to be, the bound alone decides.
No kernel may reach another device: no remote copies, remote signals or barrier semaphores. Data moves between devices by JAX's collectives and lax.ppermute only.
A program may use at most 64 MiB of HBM per device.

v0:
```python
import math

import jax
import jax.numpy as jnp
from jax import lax
from jax.sharding import PartitionSpec as P

KMAX = 6
DIFF = 2
ITERS = 2


KAPPA = 0.125
DESCENT = 0.25
HIGHEST = lax.Precision.HIGHEST


def with_halo(x, sides, width):
    for axis, dim in sides:
        peers, length = (lax.axis_size(axis), x.shape[dim])
        up = [(i, (i + 1) % peers) for i in range(peers - 1)]
        down = [(j, i) for i, j in up]
        last = lax.slice_in_dim(x, length - width, length, axis=dim)
        initial = lax.slice_in_dim(x, 0, width, axis=dim)
        before = lax.ppermute(last, axis, up)
        after = lax.ppermute(initial, axis, down)
        x = jnp.concatenate([before, x, after], axis=dim)
    return x


def from_behind(block, axis, distance):
    devices = range(lax.axis_size(axis))
    route = [(i - distance, i) for i in devices if i - distance in devices]
    return lax.ppermute(block, axis, route)


def relax(padded):
    middle = padded[:, 1:-1, :]
    beside_all = (
        padded[:, 2:, :] + padded[:, :-2, :] + jnp.roll(middle, 1, -1) + jnp.roll(middle, -1, -1)
    )
    return middle + KAPPA * (beside_all - 4.0 * middle)


def inside_mask(rows, width):
    anchor = lax.axis_index("lat") * rows - width
    global_rows = anchor + jnp.arange(rows + 2 * width, dtype=jnp.int32)
    return (global_rows >= 0) & (global_rows < rows * lax.axis_size("lat"))


def smooth(values):
    for repeat in range(DIFF):
        padded = with_halo(values, (("lat", 1),), 1)
        values = relax(padded)
    return values


def forward(state, wide_coeff, coupling, step_count):
    rows = state.shape[1]
    total = rows + 2 * KMAX
    inside_rows = inside_mask(rows, KMAX)
    current = with_halo(state, (("lat", 1),), KMAX)
    for section_index in range(KMAX):
        center = current[:, 1:-1]
        second = current[:, 2:] + current[:, :-2] - 2.0 * center
        coeff = wide_coeff[:, section_index + 1 : total - section_index - 1]
        mixed = jnp.einsum("vu,url->vrl", coupling, center, precision=HIGHEST)
        moved = center + coeff * second + mixed
        keep = inside_rows[section_index + 1 : total - section_index - 1]
        moved = jnp.where(keep[None, :, None], moved, 0.0)
        current = jnp.where(section_index < step_count, moved, center)
    state = current
    return state


def backward(state, wide_coeff, coupling, step_count):
    rows = state.shape[1]
    total = rows + 2 * KMAX
    inside_rows = inside_mask(rows, KMAX)
    current = with_halo(state, (("lat", 1),), KMAX)
    for depth_index in range(KMAX):
        section_index = KMAX - 1 - depth_index
        coeff = wide_coeff[:, depth_index : total - depth_index]
        weighted = coeff * current
        center = current[:, 1:-1]
        second = weighted[:, 2:] + weighted[:, :-2] - 2.0 * weighted[:, 1:-1]
        mixed = jnp.einsum("uv,url->vrl", coupling, center, precision=HIGHEST)
        moved = center + second + mixed
        keep = inside_rows[depth_index + 1 : total - depth_index - 1]
        moved = jnp.where(keep[None, :, None], moved, 0.0)
        current = jnp.where(section_index < step_count, moved, center)
    state = current
    return state


def local(
    ensemble,
    weights,
    diffusivity,
    coupling,
    tl_steps,
    obs_cell,
    obs_window,
    obs_value,
    obs_weight,
    error_weight,
):
    members = ensemble.shape[0] * lax.axis_size("mem")
    member_scale = 1.0 / math.sqrt(members - 1)
    control = weights[0]
    step_count = tl_steps[0]
    window = lax.axis_index("win")
    has_before = window > 0
    wide_coeff = None
    wide_coeff = with_halo(diffusivity, (("lat", 1),), KMAX)
    increment = None
    for iteration in range(ITERS):
        smoothed = smooth(control)
        partial_sum = (
            jnp.einsum("mvrl,mrl->vrl", ensemble, smoothed, precision=HIGHEST) * member_scale
        )
        increment = lax.psum_scatter(partial_sum, "mem", scatter_dimension=2, tiled=True)
        ends = forward(increment, wide_coeff, coupling, step_count)
        previous = from_behind(ends, "win", 1)
        misfit = jnp.where(has_before, error_weight[:, None, None] * (previous - increment), 0.0)
        misfit_next = from_behind(misfit, "win", -1)
        flat_state = ends.reshape(-1)
        picked = flat_state[obs_cell]
        innovation = jnp.where(obs_window == window, (picked - obs_value) * obs_weight, 0.0)
        observed = jnp.zeros_like(flat_state).at[obs_cell].add(innovation).reshape(ends.shape)
        gradient = backward(observed + misfit_next, wide_coeff, coupling, step_count) - misfit
        whole_gradient = lax.all_gather(gradient, "mem", axis=2, tiled=True)
        back_members = (
            jnp.einsum("mvrl,vrl->mrl", ensemble, whole_gradient, precision=HIGHEST) * member_scale
        )
        control = control - DESCENT * (control + smooth(back_members))
    return (control[None], increment[None])


def solution(mesh):
    return jax.shard_map(
        local,
        mesh=mesh,
        in_specs=(
            P("mem", None, "lat", None),
            P("win", "mem", "lat", None),
            P(None, "lat", "mem"),
            P(),
            P("win"),
            P(("mem", "lat")),
            P(("mem", "lat")),
            P(("mem", "lat")),
            P(("mem", "lat")),
            P(),
        ),
        out_specs=(P("win", "mem", "lat", None), P("win", None, "lat", "mem")),
        check_vma=False,
    )
```

profile of v0, /device:TPU:0, one launch (start us, length us, event | category | flops | bytes accessed | tf_op | source)
XLA Modules:
  0.0 229.3 jit_solution(13767630054365599164)
XLA Ops:
  9.4 5.6 %collective-permute-start.1 = (f32[2,1,512]{2,1,0:T(1,128)S(1)}, f32[2,1,512]{2,1,0:T(1,128)S(1)}, u32[]{:S(2)}, u32[]{:S(2)}) collective-permute-start(f32[2,1,512]{2,1,0:T(1,128)S(1)} %get-tuple-element.69), channel_id=1, source_target_pairs={{0,2},{2,4},{4,6},{1,3},{3,5},{5,7},{8,10},{10,12},{12,14},{9,11},... | collective-permute-start | bytes 12296 | tf_op jit(solution)/shard_map/ppermute | solution.py:25
  15.8 3.9 %collective-permute-start.6 = (f32[8,6,128]{2,0,1:T(8,128)S(1)}, f32[8,6,128]{2,0,1:T(8,128)S(1)}, u32[]{:S(2)}, u32[]{:S(2)}) collective-permute-start(f32[8,6,128]{2,0,1:T(8,128)S(1)} %copy.117), channel_id=1, source_target_pairs={{0,2},{2,4},{4,6},{1,3},{3,5},{5,7},{8,10},{10,12},{12,14},{9,11},... | collective-permute-start | bytes 73736 | tf_op jit(solution)/shard_map/ppermute | solution.py:25
  19.8 1.3 collective-permute-start.7
  23.9 5.2 %collective-permute-start.3 = (f32[2,1,512]{2,1,0:T(1,128)S(1)}, f32[2,1,512]{2,1,0:T(1,128)S(1)}, u32[]{:S(2)}, u32[]{:S(2)}) collective-permute-start(f32[2,1,512]{2,1,0:T(1,128)S(1)} %get-tuple-element.63), channel_id=1, source_target_pairs={{0,2},{2,4},{4,6},{1,3},{3,5},{5,7},{8,10},{10,12},{12,14},{9,11},... | collective-permute-start | bytes 12296 | tf_op jit(solution)/shard_map/ppermute | solution.py:25
  32.0 25.9 %reduce-scatter.3.cloned.1.call-done = f32[8,8,128]{2,0,1:T(8,128)} async-done(((f32[8,8,512]{2,0,1:T(8,128)}), f32[8,8,128]{2,0,1:T(8,128)}) %reduce-scatter.3.cloned.1.call-update) | async-done | bytes 32784 | tf_op jit(solution)/shard_map/reduce_scatter | solution.py:122
  58.8 3.4 %collective-permute-start.4 = (f32[8,6,128]{2,0,1:T(8,128)S(1)}, f32[8,6,128]{2,0,1:T(8,128)S(1)}, u32[]{:S(2)}, u32[]{:S(2)}) collective-permute-start(f32[8,6,128]{2,0,1:T(8,128)S(1)} %get-tuple-element.57), channel_id=1, source_target_pairs={{0,2},{2,4},{4,6},{1,3},{3,5},{5,7},{8,10},{10,12},{12,14},{9,11},... | collective-permute-start | bytes 73736 | tf_op jit(solution)/shard_map/ppermute | solution.py:25
  62.2 1.3 collective-permute-start.5
  63.7 4.2 %collective-permute-done.5 = f32[8,6,128]{2,0,1:T(8,128)S(1)} collective-permute-done((f32[8,6,128]{2,0,1:T(8,128)S(1)}, f32[8,6,128]{2,0,1:T(8,128)S(1)}, u32[]{:S(2)}, u32[]{:S(2)}) %collective-permute-start.5) | collective-permute-done | bytes 24608 | tf_op jit(solution)/shard_map/ppermute | solution.py:26
  69.1 1.3 collective-permute-start.8
  70.4 6.2 %gather_fusion = f32[1024]{0:T(1024)S(1)} fusion(f32[8192]{0:T(1024)S(1)} %bitcast.321, s32[1024]{0:T(1024)S(1)} %get-tuple-element.70), kind=kCustom, calls=%fused_computation | custom fusion | bytes 12288 | tf_op jit(solution)/shard_map/gather | solution.py:128
  78.1 5.9 %scatter_custom_fusion = f32[8192]{0:T(1024)S(1)} fusion(s32[1024]{0:T(1024)S(1)} %get-tuple-element.71, f32[1024]{0:T(1024)S(1)} %get-tuple-element.6, f32[]{:T(128)} %constant.16.clone.1), kind=kCustom, calls=%fused_computation.310 | custom fusion | flops 1024 | bytes 32772 | tf_op jit(solution)/shard_map/scatter-add | solution.py:130
  84.1 3.4 %collective-permute-start.10 = (f32[8,6,128]{2,0,1:T(8,128)S(1)}, f32[8,6,128]{2,0,1:T(8,128)S(1)}, u32[]{:S(2)}, u32[]{:S(2)}) collective-permute-start(f32[8,6,128]{2,0,1:T(8,128)S(1)} %get-tuple-element.52), channel_id=1, source_target_pairs={{0,2},{2,4},{4,6},{1,3},{3,5},{5,7},{8,10},{10,12},{12,14},{9,11},... | collective-permute-start | bytes 73736 | tf_op jit(solution)/shard_map/ppermute | solution.py:25
  87.4 1.3 collective-permute-start.11
  89.0 4.4 %collective-permute-done.11 = f32[8,6,128]{2,0,1:T(8,128)S(1)} collective-permute-done((f32[8,6,128]{2,0,1:T(8,128)S(1)}, f32[8,6,128]{2,0,1:T(8,128)S(1)}, u32[]{:S(2)}, u32[]{:S(2)}) %collective-permute-start.11) | collective-permute-done | bytes 24608 | tf_op jit(solution)/shard_map/ppermute | solution.py:26
  94.8 9.0 %all_gather.6 = f32[8,8,512]{2,0,1:T(8,128)S(1)} all-gather(f32[8,8,128]{2,0,1:T(8,128)S(1)} %fusion.34), channel_id=1, replica_groups=mesh['mem'=4,'lat'=4,'win'=2] {'mem'}, dimensions={2}, use_global_device_ids=true | all-gather | bytes 163840 | tf_op jit(solution)/shard_map/all_gather | solution.py:132
  105.3 4.5 %collective-permute-start.13 = (f32[2,1,512]{2,1,0:T(1,128)S(1)}, f32[2,1,512]{2,1,0:T(1,128)S(1)}, u32[]{:S(2)}, u32[]{:S(2)}) collective-permute-start(f32[2,1,512]{2,1,0:T(1,128)S(1)} %get-tuple-element.51), channel_id=1, source_target_pairs={{0,2},{2,4},{4,6},{1,3},{3,5},{5,7},{8,10},{10,12},{12,14},{9,11},... | collective-permute-start | bytes 12296 | tf_op jit(solution)/shard_map/ppermute | solution.py:25
  112.7 4.8 %collective-permute-start.15 = (f32[2,1,512]{2,1,0:T(1,128)S(1)}, f32[2,1,512]{2,1,0:T(1,128)S(1)}, u32[]{:S(2)}, u32[]{:S(2)}) collective-permute-start(f32[2,1,512]{2,1,0:T(1,128)S(1)} %get-tuple-element.45), channel_id=1, source_target_pairs={{0,2},{2,4},{4,6},{1,3},{3,5},{5,7},{8,10},{10,12},{12,14},{9,11},... | collective-permute-start | bytes 12296 | tf_op jit(solution)/shard_map/ppermute | solution.py:25
  120.3 4.8 %collective-permute-start.17 = (f32[2,1,512]{2,1,0:T(1,128)S(1)}, f32[2,1,512]{2,1,0:T(1,128)S(1)}, u32[]{:S(2)}, u32[]{:S(2)}) collective-permute-start(f32[2,1,512]{2,1,0:T(1,128)S(1)} %get-tuple-element.39), channel_id=1, source_target_pairs={{0,2},{2,4},{4,6},{1,3},{3,5},{5,7},{8,10},{10,12},{12,14},{9,11},... | collective-permute-start | bytes 12296 | tf_op jit(solution)/shard_map/ppermute | solution.py:25
  127.9 4.8 %collective-permute-start.19 = (f32[2,1,512]{2,1,0:T(1,128)S(1)}, f32[2,1,512]{2,1,0:T(1,128)S(1)}, u32[]{:S(2)}, u32[]{:S(2)}) collective-permute-start(f32[2,1,512]{2,1,0:T(1,128)S(1)} %get-tuple-element.33), channel_id=1, source_target_pairs={{0,2},{2,4},{4,6},{1,3},{3,5},{5,7},{8,10},{10,12},{12,14},{9,11},... | collective-permute-start | bytes 12296 | tf_op jit(solution)/shard_map/ppermute | solution.py:25
  134.9 26.1 %reduce-scatter.5.cloned.1.call-done = f32[8,8,128]{2,0,1:T(8,128)} async-done(((f32[8,8,512]{2,0,1:T(8,128)}), f32[8,8,128]{2,0,1:T(8,128)}) %reduce-scatter.5.cloned.1.call-update) | async-done | bytes 32784 | tf_op jit(solution)/shard_map/reduce_scatter | solution.py:122
  161.8 3.5 %collective-permute-start.20 = (f32[8,6,128]{2,0,1:T(8,128)S(1)}, f32[8,6,128]{2,0,1:T(8,128)S(1)}, u32[]{:S(2)}, u32[]{:S(2)}) collective-permute-start(f32[8,6,128]{2,0,1:T(8,128)S(1)} %get-tuple-element.27), channel_id=1, source_target_pairs={{0,2},{2,4},{4,6},{1,3},{3,5},{5,7},{8,10},{10,12},{12,14},{9,11},... | collective-permute-start | bytes 73736 | tf_op jit(solution)/shard_map/ppermute | solution.py:25
  165.4 1.3 collective-permute-start.21
  166.9 4.2 %collective-permute-done.21 = f32[8,6,128]{2,0,1:T(8,128)S(1)} collective-permute-done((f32[8,6,128]{2,0,1:T(8,128)S(1)}, f32[8,6,128]{2,0,1:T(8,128)S(1)}, u32[]{:S(2)}, u32[]{:S(2)}) %collective-permute-start.21) | collective-permute-done | bytes 24608 | tf_op jit(solution)/shard_map/ppermute | solution.py:26
  172.2 1.3 collective-permute-start.22
  173.5 6.2 %gather_fusion.1 = f32[1024]{0:T(1024)S(1)} fusion(f32[8192]{0:T(1024)S(1)} %bitcast.320, s32[1024]{0:T(1024)S(1)} %get-tuple-element.70), kind=kCustom, calls=%fused_computation.1 | custom fusion | bytes 12288 | tf_op jit(solution)/shard_map/gather | solution.py:128
  181.1 5.9 %scatter_custom_fusion.1 = f32[8192]{0:T(1024)S(1)} fusion(s32[1024]{0:T(1024)S(1)} %get-tuple-element.71, f32[1024]{0:T(1024)S(1)} %multiply_select_fusion.2, f32[]{:T(128)} %constant.16.clone.1), kind=kCustom, calls=%fused_computation.308 | custom fusion | flops 1024 | bytes 32772 | tf_op jit(solution)/shard_map/scatter-add | solution.py:130
  187.1 3.4 %collective-permute-start.24 = (f32[8,6,128]{2,0,1:T(8,128)S(1)}, f32[8,6,128]{2,0,1:T(8,128)S(1)}, u32[]{:S(2)}, u32[]{:S(2)}) collective-permute-start(f32[8,6,128]{2,0,1:T(8,128)S(1)} %get-tuple-element.24), channel_id=1, source_target_pairs={{0,2},{2,4},{4,6},{1,3},{3,5},{5,7},{8,10},{10,12},{12,14},{9,11},... | collective-permute-start | bytes 73736 | tf_op jit(solution)/shard_map/ppermute | solution.py:25
  190.5 1.3 collective-permute-start.25
  192.4 3.9 %collective-permute-done.25 = f32[8,6,128]{2,0,1:T(8,128)S(1)} collective-permute-done((f32[8,6,128]{2,0,1:T(8,128)S(1)}, f32[8,6,128]{2,0,1:T(8,128)S(1)}, u32[]{:S(2)}, u32[]{:S(2)}) %collective-permute-start.25) | collective-permute-done | bytes 24608 | tf_op jit(solution)/shard_map/ppermute | solution.py:26
  197.9 8.9 %all_gather.7 = f32[8,8,512]{2,0,1:T(8,128)S(1)} all-gather(f32[8,8,128]{2,0,1:T(8,128)S(1)} %fusion.27), channel_id=1, replica_groups=mesh['mem'=4,'lat'=4,'win'=2] {'mem'}, dimensions={2}, use_global_device_ids=true | all-gather | bytes 163840 | tf_op jit(solution)/shard_map/all_gather | solution.py:132
  208.3 4.5 %collective-permute-start.27 = (f32[2,1,512]{2,1,0:T(1,128)S(1)}, f32[2,1,512]{2,1,0:T(1,128)S(1)}, u32[]{:S(2)}, u32[]{:S(2)}) collective-permute-start(f32[2,1,512]{2,1,0:T(1,128)S(1)} %get-tuple-element.23), channel_id=1, source_target_pairs={{0,2},{2,4},{4,6},{1,3},{3,5},{5,7},{8,10},{10,12},{12,14},{9,11},... | collective-permute-start | bytes 12296 | tf_op jit(solution)/shard_map/ppermute | solution.py:25
  215.7 4.8 %collective-permute-start.29 = (f32[2,1,512]{2,1,0:T(1,128)S(1)}, f32[2,1,512]{2,1,0:T(1,128)S(1)}, u32[]{:S(2)}, u32[]{:S(2)}) collective-permute-start(f32[2,1,512]{2,1,0:T(1,128)S(1)} %get-tuple-element.17), channel_id=1, source_target_pairs={{0,2},{2,4},{4,6},{1,3},{3,5},{5,7},{8,10},{10,12},{12,14},{9,11},... | collective-permute-start | bytes 12296 | tf_op jit(solution)/shard_map/ppermute | solution.py:25
  (163 shorter events, 37.1 us)
Async XLA Ops:
  7.2 50.8 %reduce-scatter.3.cloned.1.call-start = ((), (), s32[]{:S(2)}) async-start(), calls=%async_computation.2 | async-start | bytes 163840 | tf_op jit(solution)/shard_map/reduce_scatter | solution.py:122
  8.1 14.3 %collective-permute-start = (f32[2,1,512]{2,1,0:T(1,128)S(1)}, f32[2,1,512]{2,1,0:T(1,128)S(1)}, u32[]{:S(2)}, u32[]{:S(2)}) collective-permute-start(f32[2,1,512]{2,1,0:T(1,128)S(1)} %get-tuple-element.68), channel_id=1, source_target_pairs={{2,0},{4,2},{6,4},{3,1},{5,3},{7,5},{10,8},{12,10},{14,12},{11,9},... | collective-permute-start | bytes 12296 | tf_op jit(solution)/shard_map/ppermute | solution.py:26
  9.4 13.1 %collective-permute-start.1 = (f32[2,1,512]{2,1,0:T(1,128)S(1)}, f32[2,1,512]{2,1,0:T(1,128)S(1)}, u32[]{:S(2)}, u32[]{:S(2)}) collective-permute-start(f32[2,1,512]{2,1,0:T(1,128)S(1)} %get-tuple-element.69), channel_id=1, source_target_pairs={{0,2},{2,4},{4,6},{1,3},{3,5},{5,7},{8,10},{10,12},{12,14},{9,11},... | collective-permute-start | bytes 12296 | tf_op jit(solution)/shard_map/ppermute | solution.py:25
  15.8 15.5 %collective-permute-start.6 = (f32[8,6,128]{2,0,1:T(8,128)S(1)}, f32[8,6,128]{2,0,1:T(8,128)S(1)}, u32[]{:S(2)}, u32[]{:S(2)}) collective-permute-start(f32[8,6,128]{2,0,1:T(8,128)S(1)} %copy.117), channel_id=1, source_target_pairs={{0,2},{2,4},{4,6},{1,3},{3,5},{5,7},{8,10},{10,12},{12,14},{9,11},... | collective-permute-start | bytes 73736 | tf_op jit(solution)/shard_map/ppermute | solution.py:25
  19.8 42.4 %collective-permute-start.7 = (f32[8,6,128]{2,0,1:T(8,128)S(1)}, f32[8,6,128]{2,0,1:T(8,128)S(1)}, u32[]{:S(2)}, u32[]{:S(2)}) collective-permute-start(f32[8,6,128]{2,0,1:T(8,128)S(1)} %copy.118), channel_id=1, source_target_pairs={{2,0},{4,2},{6,4},{3,1},{5,3},{7,5},{10,8},{12,10},{14,12},{11,9},... | collective-permute-start | bytes 73736 | tf_op jit(solution)/shard_map/ppermute | solution.py:26
  22.6 6.6 %collective-permute-start.2 = (f32[2,1,512]{2,1,0:T(1,128)S(1)}, f32[2,1,512]{2,1,0:T(1,128)S(1)}, u32[]{:S(2)}, u32[]{:S(2)}) collective-permute-start(f32[2,1,512]{2,1,0:T(1,128)S(1)} %get-tuple-element.62), channel_id=1, source_target_pairs={{2,0},{4,2},{6,4},{3,1},{5,3},{7,5},{10,8},{12,10},{14,12},{11,9},... | collective-permute-start | bytes 12296 | tf_op jit(solution)/shard_map/ppermute | solution.py:26
  23.9 6.5 %collective-permute-start.3 = (f32[2,1,512]{2,1,0:T(1,128)S(1)}, f32[2,1,512]{2,1,0:T(1,128)S(1)}, u32[]{:S(2)}, u32[]{:S(2)}) collective-permute-start(f32[2,1,512]{2,1,0:T(1,128)S(1)} %get-tuple-element.63), channel_id=1, source_target_pairs={{0,2},{2,4},{4,6},{1,3},{3,5},{5,7},{8,10},{10,12},{12,14},{9,11},... | collective-permute-start | bytes 12296 | tf_op jit(solution)/shard_map/ppermute | solution.py:25
  31.3 129.7 %reduce-scatter.5.cloned.1.call-start = ((), (), s32[]{:S(2)}) async-start(), calls=%async_computation.3 | async-start | bytes 163840 | tf_op jit(solution)/shard_map/reduce_scatter | solution.py:122
  58.8 4.9 %collective-permute-start.4 = (f32[8,6,128]{2,0,1:T(8,128)S(1)}, f32[8,6,128]{2,0,1:T(8,128)S(1)}, u32[]{:S(2)}, u32[]{:S(2)}) collective-permute-start(f32[8,6,128]{2,0,1:T(8,128)S(1)} %get-tuple-element.57), channel_id=1, source_target_pairs={{0,2},{2,4},{4,6},{1,3},{3,5},{5,7},{8,10},{10,12},{12,14},{9,11},... | collective-permute-start | bytes 73736 | tf_op jit(solution)/shard_map/ppermute | solution.py:25
  62.2 5.7 %collective-permute-start.5 = (f32[8,6,128]{2,0,1:T(8,128)S(1)}, f32[8,6,128]{2,0,1:T(8,128)S(1)}, u32[]{:S(2)}, u32[]{:S(2)}) collective-permute-start(f32[8,6,128]{2,0,1:T(8,128)S(1)} %get-tuple-element.56), channel_id=1, source_target_pairs={{2,0},{4,2},{6,4},{3,1},{5,3},{7,5},{10,8},{12,10},{14,12},{11,9},... | collective-permute-start | bytes 73736 | tf_op jit(solution)/shard_map/ppermute | solution.py:26
  69.1 7.6 %collective-permute-start.8 = (f32[8,8,128]{2,0,1:T(8,128)S(1)}, f32[8,8,128]{2,0,1:T(8,128)S(1)}, u32[]{:S(2)}, u32[]{:S(2)}) collective-permute-start(f32[8,8,128]{2,0,1:T(8,128)S(1)} %fusion.37), channel_id=1, source_target_pairs={{0,1},{2,3},{4,5},{6,7},{8,9},{10,11},{12,13},{14,15},{16,17},{18,... | collective-permute-start | bytes 98312 | tf_op jit(solution)/shard_map/ppermute | solution.py:34
  76.7 7.3 %collective-permute-start.9 = (f32[8,8,128]{2,0,1:T(8,128)S(1)}, f32[8,8,128]{2,0,1:T(8,128)S(1)}, u32[]{:S(2)}, u32[]{:S(2)}) collective-permute-start(f32[8,8,128]{2,0,1:T(8,128)S(1)} %multiply_select_fusion.1), channel_id=1, source_target_pairs={{1,0},{3,2},{5,4},{7,6},{9,8},{11,10},{13,12},{15,14},{17,16},{19,... | collective-permute-start | bytes 98312 | tf_op jit(solution)/shard_map/ppermute | solution.py:34
  84.1 4.9 %collective-permute-start.10 = (f32[8,6,128]{2,0,1:T(8,128)S(1)}, f32[8,6,128]{2,0,1:T(8,128)S(1)}, u32[]{:S(2)}, u32[]{:S(2)}) collective-permute-start(f32[8,6,128]{2,0,1:T(8,128)S(1)} %get-tuple-element.52), channel_id=1, source_target_pairs={{0,2},{2,4},{4,6},{1,3},{3,5},{5,7},{8,10},{10,12},{12,14},{9,11},... | collective-permute-start | bytes 73736 | tf_op jit(solution)/shard_map/ppermute | solution.py:25
  87.4 5.9 %collective-permute-start.11 = (f32[8,6,128]{2,0,1:T(8,128)S(1)}, f32[8,6,128]{2,0,1:T(8,128)S(1)}, u32[]{:S(2)}, u32[]{:S(2)}) collective-permute-start(f32[8,6,128]{2,0,1:T(8,128)S(1)} %get-tuple-element.53), channel_id=1, source_target_pairs={{2,0},{4,2},{6,4},{3,1},{5,3},{7,5},{10,8},{12,10},{14,12},{11,9},... | collective-permute-start | bytes 73736 | tf_op jit(solution)/shard_map/ppermute | solution.py:26
  104.0 5.9 %collective-permute-start.12 = (f32[2,1,512]{2,1,0:T(1,128)S(1)}, f32[2,1,512]{2,1,0:T(1,128)S(1)}, u32[]{:S(2)}, u32[]{:S(2)}) collective-permute-start(f32[2,1,512]{2,1,0:T(1,128)S(1)} %get-tuple-element.50), channel_id=1, source_target_pairs={{2,0},{4,2},{6,4},{3,1},{5,3},{7,5},{10,8},{12,10},{14,12},{11,9},... | collective-permute-start | bytes 12296 | tf_op jit(solution)/shard_map/ppermute | solution.py:26
  105.3 5.9 %collective-permute-start.13 = (f32[2,1,512]{2,1,0:T(1,128)S(1)}, f32[2,1,512]{2,1,0:T(1,128)S(1)}, u32[]{:S(2)}, u32[]{:S(2)}) collective-permute-start(f32[2,1,512]{2,1,0:T(1,128)S(1)} %get-tuple-element.51), channel_id=1, source_target_pairs={{0,2},{2,4},{4,6},{1,3},{3,5},{5,7},{8,10},{10,12},{12,14},{9,11},... | collective-permute-start | bytes 12296 | tf_op jit(solution)/shard_map/ppermute | solution.py:25
  111.4 6.2 %collective-permute-start.14 = (f32[2,1,512]{2,1,0:T(1,128)S(1)}, f32[2,1,512]{2,1,0:T(1,128)S(1)}, u32[]{:S(2)}, u32[]{:S(2)}) collective-permute-start(f32[2,1,512]{2,1,0:T(1,128)S(1)} %get-tuple-element.44), channel_id=1, source_target_pairs={{2,0},{4,2},{6,4},{3,1},{5,3},{7,5},{10,8},{12,10},{14,12},{11,9},... | collective-permute-start | bytes 12296 | tf_op jit(solution)/shard_map/ppermute | solution.py:26
  112.7 6.1 %collective-permute-start.15 = (f32[2,1,512]{2,1,0:T(1,128)S(1)}, f32[2,1,512]{2,1,0:T(1,128)S(1)}, u32[]{:S(2)}, u32[]{:S(2)}) collective-permute-start(f32[2,1,512]{2,1,0:T(1,128)S(1)} %get-tuple-element.45), channel_id=1, source_target_pairs={{0,2},{2,4},{4,6},{1,3},{3,5},{5,7},{8,10},{10,12},{12,14},{9,11},... | collective-permute-start | bytes 12296 | tf_op jit(solution)/shard_map/ppermute | solution.py:25
  119.0 6.2 %collective-permute-start.16 = (f32[2,1,512]{2,1,0:T(1,128)S(1)}, f32[2,1,512]{2,1,0:T(1,128)S(1)}, u32[]{:S(2)}, u32[]{:S(2)}) collective-permute-start(f32[2,1,512]{2,1,0:T(1,128)S(1)} %get-tuple-element.38), channel_id=1, source_target_pairs={{2,0},{4,2},{6,4},{3,1},{5,3},{7,5},{10,8},{12,10},{14,12},{11,9},... | collective-permute-start | bytes 12296 | tf_op jit(solution)/shard_map/ppermute | solution.py:26
  120.3 6.1 %collective-permute-start.17 = (f32[2,1,512]{2,1,0:T(1,128)S(1)}, f32[2,1,512]{2,1,0:T(1,128)S(1)}, u32[]{:S(2)}, u32[]{:S(2)}) collective-permute-start(f32[2,1,512]{2,1,0:T(1,128)S(1)} %get-tuple-element.39), channel_id=1, source_target_pairs={{0,2},{2,4},{4,6},{1,3},{3,5},{5,7},{8,10},{10,12},{12,14},{9,11},... | collective-permute-start | bytes 12296 | tf_op jit(solution)/shard_map/ppermute | solution.py:25
  126.6 6.2 %collective-permute-start.18 = (f32[2,1,512]{2,1,0:T(1,128)S(1)}, f32[2,1,512]{2,1,0:T(1,128)S(1)}, u32[]{:S(2)}, u32[]{:S(2)}) collective-permute-start(f32[2,1,512]{2,1,0:T(1,128)S(1)} %get-tuple-element.32), channel_id=1, source_target_pairs={{2,0},{4,2},{6,4},{3,1},{5,3},{7,5},{10,8},{12,10},{14,12},{11,9},... | collective-permute-start | bytes 12296 | tf_op jit(solution)/shard_map/ppermute | solution.py:26
  127.9 6.1 %collective-permute-start.19 = (f32[2,1,512]{2,1,0:T(1,128)S(1)}, f32[2,1,512]{2,1,0:T(1,128)S(1)}, u32[]{:S(2)}, u32[]{:S(2)}) collective-permute-start(f32[2,1,512]{2,1,0:T(1,128)S(1)} %get-tuple-element.33), channel_id=1, source_target_pairs={{0,2},{2,4},{4,6},{1,3},{3,5},{5,7},{8,10},{10,12},{12,14},{9,11},... | collective-permute-start | bytes 12296 | tf_op jit(solution)/shard_map/ppermute | solution.py:25
  161.8 5.0 %collective-permute-start.20 = (f32[8,6,128]{2,0,1:T(8,128)S(1)}, f32[8,6,128]{2,0,1:T(8,128)S(1)}, u32[]{:S(2)}, u32[]{:S(2)}) collective-permute-start(f32[8,6,128]{2,0,1:T(8,128)S(1)} %get-tuple-element.27), channel_id=1, source_target_pairs={{0,2},{2,4},{4,6},{1,3},{3,5},{5,7},{8,10},{10,12},{12,14},{9,11},... | collective-permute-start | bytes 73736 | tf_op jit(solution)/shard_map/ppermute | solution.py:25
  165.4 5.7 %collective-permute-start.21 = (f32[8,6,128]{2,0,1:T(8,128)S(1)}, f32[8,6,128]{2,0,1:T(8,128)S(1)}, u32[]{:S(2)}, u32[]{:S(2)}) collective-permute-start(f32[8,6,128]{2,0,1:T(8,128)S(1)} %get-tuple-element.26), channel_id=1, source_target_pairs={{2,0},{4,2},{6,4},{3,1},{5,3},{7,5},{10,8},{12,10},{14,12},{11,9},... | collective-permute-start | bytes 73736 | tf_op jit(solution)/shard_map/ppermute | solution.py:26
  172.2 7.5 %collective-permute-start.22 = (f32[8,8,128]{2,0,1:T(8,128)S(1)}, f32[8,8,128]{2,0,1:T(8,128)S(1)}, u32[]{:S(2)}, u32[]{:S(2)}) collective-permute-start(f32[8,8,128]{2,0,1:T(8,128)S(1)} %fusion.30), channel_id=1, source_target_pairs={{0,1},{2,3},{4,5},{6,7},{8,9},{10,11},{12,13},{14,15},{16,17},{18,... | collective-permute-start | bytes 98312 | tf_op jit(solution)/shard_map/ppermute | solution.py:34
  179.8 7.3 %collective-permute-start.23 = (f32[8,8,128]{2,0,1:T(8,128)S(1)}, f32[8,8,128]{2,0,1:T(8,128)S(1)}, u32[]{:S(2)}, u32[]{:S(2)}) collective-permute-start(f32[8,8,128]{2,0,1:T(8,128)S(1)} %multiply_select_fusion), channel_id=1, source_target_pairs={{1,0},{3,2},{5,4},{7,6},{9,8},{11,10},{13,12},{15,14},{17,16},{19,... | collective-permute-start | bytes 98312 | tf_op jit(solution)/shard_map/ppermute | solution.py:34
  187.1 5.3 %collective-permute-start.24 = (f32[8,6,128]{2,0,1:T(8,128)S(1)}, f32[8,6,128]{2,0,1:T(8,128)S(1)}, u32[]{:S(2)}, u32[]{:S(2)}) collective-permute-start(f32[8,6,128]{2,0,1:T(8,128)S(1)} %get-tuple-element.24), channel_id=1, source_target_pairs={{0,2},{2,4},{4,6},{1,3},{3,5},{5,7},{8,10},{10,12},{12,14},{9,11},... | collective-permute-start | bytes 73736 | tf_op jit(solution)/shard_map/ppermute | solution.py:25
  190.5 5.9 %collective-permute-start.25 = (f32[8,6,128]{2,0,1:T(8,128)S(1)}, f32[8,6,128]{2,0,1:T(8,128)S(1)}, u32[]{:S(2)}, u32[]{:S(2)}) collective-permute-start(f32[8,6,128]{2,0,1:T(8,128)S(1)} %get-tuple-element.25), channel_id=1, source_target_pairs={{2,0},{4,2},{6,4},{3,1},{5,3},{7,5},{10,8},{12,10},{14,12},{11,9},... | collective-permute-start | bytes 73736 | tf_op jit(solution)/shard_map/ppermute | solution.py:26
  207.0 5.9 %collective-permute-start.26 = (f32[2,1,512]{2,1,0:T(1,128)S(1)}, f32[2,1,512]{2,1,0:T(1,128)S(1)}, u32[]{:S(2)}, u32[]{:S(2)}) collective-permute-start(f32[2,1,512]{2,1,0:T(1,128)S(1)} %get-tuple-element.22), channel_id=1, source_target_pairs={{2,0},{4,2},{6,4},{3,1},{5,3},{7,5},{10,8},{12,10},{14,12},{11,9},... | collective-permute-start | bytes 12296 | tf_op jit(solution)/shard_map/ppermute | solution.py:26
  208.3 5.9 %collective-permute-start.27 = (f32[2,1,512]{2,1,0:T(1,128)S(1)}, f32[2,1,512]{2,1,0:T(1,128)S(1)}, u32[]{:S(2)}, u32[]{:S(2)}) collective-permute-start(f32[2,1,512]{2,1,0:T(1,128)S(1)} %get-tuple-element.23), channel_id=1, source_target_pairs={{0,2},{2,4},{4,6},{1,3},{3,5},{5,7},{8,10},{10,12},{12,14},{9,11},... | collective-permute-start | bytes 12296 | tf_op jit(solution)/shard_map/ppermute | solution.py:25
  214.4 6.2 %collective-permute-start.28 = (f32[2,1,512]{2,1,0:T(1,128)S(1)}, f32[2,1,512]{2,1,0:T(1,128)S(1)}, u32[]{:S(2)}, u32[]{:S(2)}) collective-permute-start(f32[2,1,512]{2,1,0:T(1,128)S(1)} %get-tuple-element.16), channel_id=1, source_target_pairs={{2,0},{4,2},{6,4},{3,1},{5,3},{7,5},{10,8},{12,10},{14,12},{11,9},... | collective-permute-start | bytes 12296 | tf_op jit(solution)/shard_map/ppermute | solution.py:26
  215.7 6.1 %collective-permute-start.29 = (f32[2,1,512]{2,1,0:T(1,128)S(1)}, f32[2,1,512]{2,1,0:T(1,128)S(1)}, u32[]{:S(2)}, u32[]{:S(2)}) collective-permute-start(f32[2,1,512]{2,1,0:T(1,128)S(1)} %get-tuple-element.17), channel_id=1, source_target_pairs={{0,2},{2,4},{4,6},{1,3},{3,5},{5,7},{8,10},{10,12},{12,14},{9,11},... | collective-permute-start | bytes 12296 | tf_op jit(solution)/shard_map/ppermute | solution.py:25
  (11 other events, 94.1 us)
Sparse Core Ops, SparseCore 0:
  31.4 26.5 reduce-scatter.2
  135.0 25.9 reduce-scatter.4
where the time goes:
time: 231 us; the launch traced here: 229 us
  starting transfers between devices  78.6 us (34%)
  waiting for transfers between devices  78.1 us (34%)
  local copies, waits for them, and re-layouts  18.9 us (8%)
  blocking collectives  17.9 us (8%)
  between operations  15.7 us (7%)
  other arithmetic  15 us (6%)
  matrix products  5.13 us (2%)
    ppermute x13, starting transfers between devices, with_halo(): before = lax.ppermute(last, axis, up)  56.7 us
    reduce_scatter x2, waiting for transfers between devices, local(): lax.psum_scatter(partial_sum, 'mem', scatter_dimension=2, tiled=True)  52.1 us
    all_gather x2, blocking collectives, local(): whole_gradient = lax.all_gather(gradient, 'mem', axis=2, tiled=True)  17.9 us
    ppermute x13, waiting for transfers between devices, with_halo(): after = lax.ppermute(initial, axis, down)  16.8 us
    ppermute x13, starting transfers between devices, with_halo(): after = lax.ppermute(initial, axis, down)  16.7 us
    gather x2, local copies, waits for them, and re-layouts, local(): picked = flat_state[obs_cell]  12.3 us
    scatter-add x2, other arithmetic, local(): jnp.zeros_like(flat_state).at[obs_cell].add(innovation).reshape(ends.shape)  11.9 us
    ppermute x13, waiting for transfers between devices, with_halo(): before = lax.ppermute(last, axis, up)  9.22 us
  transfers between devices with their start and end apart: 32, of which 16 were waited for; matrix products, arithmetic and copies ran while one was open for 13% of the time, Pallas kernels for 0%

commit v1 on v0

v1 whole, which is shorter than its diff:
```python
import math

import jax
import jax.numpy as jnp
from jax import lax
from jax.experimental import pallas as pl
from jax.experimental.pallas import tpu as pltpu
from jax.sharding import PartitionSpec as P

KMAX = 6
DIFF = 2
ITERS = 2
KAPPA = 0.125
DESCENT = 0.25

ROWS = 8
LANES = 128
SPAN = 32
GROUPS = LANES // SPAN


def roll(x, shift, axis):
    shift %= x.shape[axis]
    return x if shift == 0 else pltpu.roll(x, shift, axis)


def lane_ids():
    return lax.broadcasted_iota(jnp.int32, (ROWS, LANES), 1)


def pad4(units):
    return list(units) + [jnp.zeros_like(units[0])] * (GROUPS - len(units))


def exchange4(x):
    group = lane_ids() // SPAN
    low, even = group < 2, group % 2 == 0
    a = [jnp.where(low, x[u], roll(x[u + 2], 64, 1)) for u in range(2)]
    b = [jnp.where(low, roll(x[u], 64, 1), x[u + 2]) for u in range(2)]
    out = []
    for first, second in (a, b):
        out.append(jnp.where(even, first, roll(second, SPAN, 1)))
        out.append(jnp.where(even, roll(first, -SPAN, 1), second))
    return out


def windows(units, own):
    halo, phases, length = (SPAN - own) // 2, SPAN // own, units[0].shape[1]
    for phase in range(phases):
        moved = pad4([roll(u, halo - own * phase, 1) for u in units])
        for tile in range(length // LANES):
            parts = exchange4([m[:, tile * LANES : (tile + 1) * LANES] for m in moved])
            for q, part in enumerate(parts):
                yield (tile * GROUPS + q) * phases + phase, part


class Sizes:
    def __init__(self, mesh_shape, members_here, variables, lon, obs_here):
        self.mem, self.lat, self.win = (mesh_shape[a] for a in ("mem", "lat", "win"))
        self.devices = self.mem * self.lat * self.win
        self.members_here, self.variables, self.lon = members_here, variables, lon
        self.members = members_here * self.mem
        self.vars_here = variables // self.win
        self.own = lon // self.devices
        self.halo = (SPAN - self.own) // 2
        self.tiles = self.lat // 2
        self.pairs = self.win // 2
        self.obs_rows = obs_here // self.win // LANES
        self.ens_regs = pl.cdiv(members_here * self.vars_here, GROUPS)
        self.dif_regs = pl.cdiv(self.vars_here, GROUPS)
        self.obs_regs = pl.cdiv(4 * self.obs_rows, ROWS)
        self.dif_at = ROWS * self.ens_regs
        self.wts_at = self.dif_at + ROWS * self.dif_regs
        self.obs_at = self.wts_at + ROWS
        self.chunk = self.obs_at + ROWS * self.obs_regs
        assert lon // self.mem == LANES and members_here < GROUPS
        assert self.halo >= 2 * DIFF * ITERS
        assert self.lat % 2 == 0 and self.win % 2 == 0 and variables % self.win == 0
        assert SPAN % self.own == 0 and variables * self.own <= LANES
        assert obs_here % (self.win * LANES) == 0


def pack_kernel(z, steps, ens, wts, dif, cell, window, value, weight, out, obs):
    k = lax.axis_index("win")
    units = [ens[m, k * z.vars_here + v] for m in range(z.members_here) for v in range(z.vars_here)]
    for reg in range(z.ens_regs):
        for d, part in windows(units[reg * GROUPS : (reg + 1) * GROUPS], z.own):
            out[d, reg * ROWS : (reg + 1) * ROWS, :] = part
    per_block = LANES // z.own
    for reg in range(z.dif_regs):
        mine = range(reg * GROUPS, min(z.vars_here, (reg + 1) * GROUPS))
        at = z.dif_at + reg * ROWS
        for d, part in windows([dif[k * z.vars_here + v] for v in mine], z.own):
            for block in range(z.mem):
                out[block * per_block + d, at : at + ROWS, :] = part
    count = jnp.full((ROWS, LANES), steps[0], jnp.int32).astype(jnp.float32)
    holds_weights = lane_ids() // SPAN < z.members_here
    for d, part in windows([wts[0, m] for m in range(z.members_here)], z.own):
        out[d, z.wts_at : z.wts_at + ROWS, :] = jnp.where(holds_weights, part, count)
    n = z.obs_rows
    for a, ref in enumerate((cell, window, value, weight)):
        rows = ref[0:n, :]
        for other in range(1, z.win):
            rows = jnp.where(k == other, ref[other * n : (other + 1) * n, :], rows)
        obs[a * n : (a + 1) * n, :] = rows.astype(jnp.float32)
    table = obs[...]
    for d in range(z.devices):
        out[d, z.obs_at :, :] = table


def spread4(first, second):
    group = lane_ids() // SPAN
    low, even = group < 2, group % 2 == 0
    a = jnp.where(even, first, roll(second, SPAN, 1))
    b = jnp.where(even, roll(first, -SPAN, 1), second)
    a2, b2 = roll(a, 64, 1), roll(b, 64, 1)
    return [jnp.where(low, a, a2), jnp.where(low, b, b2), jnp.where(low, a2, a), jnp.where(low, b2, b)]


def place(pieces, width):
    target = lane_ids() // width
    out = None
    for g, (x, lane) in enumerate(pieces):
        moved = roll(x, width * g - lane, 1)
        out = moved if out is None else jnp.where(target == g, moved, out)
    return out


def split3(x):
    high = x.astype(jnp.bfloat16).astype(jnp.float32)
    middle = (x - high).astype(jnp.bfloat16).astype(jnp.float32)
    return high, middle, x - high - middle


def descend_kernel(z, scale, coup, error_weight, recv, out, ens, dif, slope, bias):
    i, j, k = (lax.axis_index(a) for a in ("mem", "lat", "win"))
    d = (i * z.lat + j) * z.win + k
    start = lax.rem(d * z.own - z.halo + z.lon, z.lon)
    left = lax.div(start, LANES)
    right = lax.div(lax.rem(start + SPAN - 1, z.lon), LANES)
    lanes = lane_ids()
    sub = lax.broadcasted_iota(jnp.int32, (ROWS, LANES), 0)
    group = lanes // SPAN
    upper = group % 2 == 0
    in_left = start + lanes % SPAN < (left + 1) * LANES
    T, NV, M = z.tiles, z.variables, z.members

    def source(mem, lat, win):
        return (mem * z.lat + lat) * z.win + win

    for mem in range(z.mem):
        for win in range(z.win):
            for reg in range(z.ens_regs):
                for t in range(T):
                    got = spread4(*(recv[source(mem, h * T + t, win), reg * ROWS : (reg + 1) * ROWS, :] for h in range(2)))
                    for u, part in enumerate(got):
                        unit = reg * GROUPS + u
                        if unit < z.members_here * z.vars_here:
                            m = mem * z.members_here + unit // z.vars_here
                            v = win * z.vars_here + unit % z.vars_here
                            ens[m, v, t] = part
    for win in range(z.win):
        for reg in range(z.dif_regs):
            rows = pl.ds(z.dif_at + reg * ROWS, ROWS)
            for t in range(T):
                both = [
                    jnp.where(in_left, recv[source(left, h * T + t, win), rows, :], recv[source(right, h * T + t, win), rows, :])
                    for h in range(2)
                ]
                for u, part in enumerate(spread4(*both)):
                    if reg * GROUPS + u < z.vars_here:
                        dif[win * z.vars_here + reg * GROUPS + u, t] = part

    def weights_of(mem, lat, win):
        return recv[source(mem, lat, win), z.wts_at : z.wts_at + ROWS, :]

    control = []
    for m in range(M):
        mem, unit = divmod(m, z.members_here)
        control.append([
            [
                place([(weights_of(mem, h * T + t, 2 * p + w), SPAN * unit) for w in range(2) for h in range(2)], SPAN)
                for t in range(T)
            ]
            for p in range(z.pairs)
        ])
    counts = [
        place([(weights_of(0, 0, 2 * p + w), SPAN * z.members_here) for w in range(2) for h in range(2)], SPAN).astype(jnp.int32)
        for p in range(z.pairs)
    ]

    row_id = lax.broadcasted_iota(jnp.int32, (NV * ROWS, LANES), 0)
    key_id = lax.broadcasted_iota(jnp.int32, (z.win * SPAN, LANES), 0)
    n = z.obs_rows
    for lat in range(z.lat):
        rows_hot, parts = [], [[] for _ in range(3)]
        for side, block in enumerate((left, right)):
            for win in range(z.win):
                table = recv[source(block, lat, win), z.obs_at :, :]
                where = table[0:n, :].astype(jnp.int32)
                weight = table[3 * n : 4 * n, :]
                weighted = weight * table[2 * n : 3 * n, :]
                lane = block * LANES + where % LANES - start
                lane = jnp.where(lane < 0, lane + z.lon, lane)
                inside = lane < SPAN
                if side == 1:
                    inside &= left != right
                key = jnp.where(inside, table[n : 2 * n, :].astype(jnp.int32) * SPAN + lane, -1)
                row = where // LANES
                splits = list(zip(split3(weight), split3(weighted)))
                for x in range(n):
                    one = slice(x, x + 1)
                    hit = jnp.broadcast_to(key[one], key_id.shape) == key_id
                    rows_hot.append(jnp.where(jnp.broadcast_to(row[one], row_id.shape) == row_id, 1.0, 0.0).astype(jnp.bfloat16))
                    for part, pair in zip(parts, splits):
                        part.append(
                            jnp.concatenate(
                                [jnp.where(hit, jnp.broadcast_to(y[one], hit.shape), 0.0).astype(jnp.bfloat16) for y in pair], 0
                            )
                        )
        hot = jnp.concatenate(rows_hot, 1)
        total = 0.0
        for part in reversed(parts):
            total += lax.dot_general(
                hot, jnp.concatenate(part, 1), (((1,), (1,)), ((), ())), preferred_element_type=jnp.float32
            )
        h, t = divmod(lat, T)
        for q, field in enumerate((slope, bias)):
            for p in range(z.pairs):
                for w in range(2):
                    lane = (q * z.win + 2 * p + w) * SPAN
                    tile, at = divmod(lane, LANES)
                    mine = group == 2 * w + h
                    for v in range(NV):
                        x = total[v * ROWS : (v + 1) * ROWS, tile * LANES : (tile + 1) * LANES]
                        x = roll(x, SPAN * (2 * w + h) - at, 1)
                        if w == 0 and h == 0:
                            field[p, v, t] = x
                        else:
                            field[p, v, t] = jnp.where(mine, x, field[p, v, t])

    first, last = sub == 0, sub == ROWS - 1

    def beside(x):
        down = [roll(a, 1, 0) for a in x]
        up = [roll(a, -1, 0) for a in x]
        before_first = jnp.where(upper, 0.0, roll(down[T - 1], SPAN, 1))
        after_last = jnp.where(upper, roll(up[0], -SPAN, 1), 0.0)
        return [
            jnp.where(first, down[t - 1] if t else before_first, down[t])
            + jnp.where(last, up[t + 1] if t < T - 1 else after_last, up[t])
            for t in range(T)
        ]

    def smooth(x):
        for _ in range(DIFF):
            x = [
                a + KAPPA * (rows + roll(a, 1, 1) + roll(a, -1, 1) - 4.0 * a)
                for a, rows in zip(x, beside(x))
            ]
        return x

    def weigh(terms):
        total = None
        for factor, x in terms:
            total = factor * x if total is None else total + factor * x
        return total

    def forward(state, p, most):
        def step(section, flat):
            u = [list(flat[v * T : (v + 1) * T]) for v in range(NV)]
            on = section < counts[p]
            moved = []
            for v in range(NV):
                near = beside(u[v])
                for t in range(T):
                    x = u[v][t]
                    y = x + dif[v, t] * (near[t] - 2.0 * x) + weigh((coup[v, w], u[w][t]) for w in range(NV))
                    moved.append(jnp.where(on, y, x))
            return tuple(moved)

        flat = lax.fori_loop(0, most, step, tuple(x for v in state for x in v))
        return [list(flat[v * T : (v + 1) * T]) for v in range(NV)]

    def backward(state, p, most):
        def step(section, flat):
            u = [list(flat[v * T : (v + 1) * T]) for v in range(NV)]
            on = section < counts[p]
            moved = []
            for v in range(NV):
                weighted = [dif[v, t] * u[v][t] for t in range(T)]
                near = beside(weighted)
                for t in range(T):
                    x = u[v][t]
                    y = x + (near[t] - 2.0 * weighted[t]) + weigh((coup[w, v], u[w][t]) for w in range(NV))
                    moved.append(jnp.where(on, y, x))
            return tuple(moved)

        flat = lax.fori_loop(0, most, step, tuple(x for v in state for x in v))
        return [list(flat[v * T : (v + 1) * T]) for v in range(NV)]

    most = [jnp.max(c) for c in counts]
    later = group >= 2
    zero = jnp.zeros((ROWS, LANES), jnp.float32)
    for _ in range(ITERS):
        increment, ends = [], []
        smoothed = [[smooth(control[m][p]) for p in range(z.pairs)] for m in range(M)]
        for p in range(z.pairs):
            increment.append(
                [[weigh((ens[m, v, t], smoothed[m][p][t]) for m in range(M)) * scale for t in range(T)] for v in range(NV)]
            )
            ends.append(forward(increment[p], p, most[p]))
        misfit = []
        for p in range(z.pairs):
            misfit.append([])
            for v in range(NV):
                misfit[p].append([])
                for t in range(T):
                    before = roll(ends[p][v][t], 64, 1)
                    if p:
                        before = jnp.where(later, before, roll(ends[p - 1][v][t], 64, 1))
                    x = error_weight[v] * (before - increment[p][v][t])
                    misfit[p][v].append(x if p else jnp.where(later, x, 0.0))
        members_back = [[] for _ in range(M)]
        for p in range(z.pairs):
            forcing = []
            for v in range(NV):
                forcing.append([])
                for t in range(T):
                    after = roll(misfit[p + 1][v][t], 64, 1) if p + 1 < z.pairs else zero
                    after = jnp.where(later, after, roll(misfit[p][v][t], 64, 1))
                    forcing[v].append(slope[p, v, t] * ends[p][v][t] - bias[p, v, t] + after)
            adjoint = backward(forcing, p, most[p])
            gradient = [[adjoint[v][t] - misfit[p][v][t] for t in range(T)] for v in range(NV)]
            for m in range(M):
                members_back[m].append(
                    [weigh((ens[m, v, t], gradient[v][t]) for v in range(NV)) * scale for t in range(T)]
                )
        for m in range(M):
            for p in range(z.pairs):
                pulled = smooth(members_back[m][p])
                control[m][p] = [c - DESCENT * (c + x) for c, x in zip(control[m][p], pulled)]

    for lat in range(z.lat):
        h, t = divmod(lat, T)
        for win in range(z.win):
            p, w = divmod(win, 2)
            lane = SPAN * (2 * w + h) + z.halo
            grown = place([(increment[p][v][t], lane) for v in range(NV)], z.own)
            for mem in range(z.mem):
                to = source(mem, lat, win)
                mine = [control[mem * z.members_here + m][p][t] for m in range(z.members_here)]
                out[to, 0:ROWS, :] = place([(x, lane) for x in mine], z.own)
                out[to, ROWS : 2 * ROWS, :] = grown


def unpack_kernel(z, recv, control, increment):
    per_tile = LANES // z.own
    for m in range(z.members_here):
        for tile in range(z.lon // LANES):
            control[0, m, :, tile * LANES : (tile + 1) * LANES] = place(
                [(recv[tile * per_tile + q, 0:ROWS, :], z.own * m) for q in range(per_tile)], z.own
            )
    i = lax.axis_index("mem")
    for v in range(z.variables):
        increment[0, v] = place(
            [(recv[i * per_tile + q, ROWS : 2 * ROWS, :], z.own * v) for q in range(per_tile)], z.own
        )


def solution(mesh):
    smem = pl.BlockSpec(memory_space=pltpu.SMEM)
    vmem = pl.BlockSpec(memory_space=pltpu.VMEM)
    f32 = jnp.float32

    def local(ensemble, weights, diffusivity, coupling, tl_steps, obs_cell, obs_window, obs_value, obs_weight, error_weight):
        z = Sizes(mesh.shape, ensemble.shape[0], ensemble.shape[1], ensemble.shape[3], obs_cell.shape[0])
        scale = 1.0 / math.sqrt(z.members - 1)
        axes = ("mem", "lat", "win")
        tables = [x.reshape(-1, LANES) for x in (obs_cell, obs_window, obs_value, obs_weight)]
        sent = pl.pallas_call(
            lambda *refs: pack_kernel(z, *refs),
            out_shape=jax.ShapeDtypeStruct((z.devices, z.chunk, LANES), f32),
            in_specs=[smem] + [vmem] * 7,
            out_specs=vmem,
            scratch_shapes=[pltpu.VMEM((ROWS * z.obs_regs, LANES), f32)],
            name="pack",
        )(tl_steps, ensemble, weights, diffusivity, *tables)
        got = lax.all_to_all(sent, axes, 0, 0)
        field = pltpu.VMEM((z.pairs, z.variables, z.tiles, ROWS, LANES), f32)
        back = pl.pallas_call(
            lambda *refs: descend_kernel(z, scale, *refs),
            out_shape=jax.ShapeDtypeStruct((z.devices, 2 * ROWS, LANES), f32),
            in_specs=[smem, smem, vmem],
            out_specs=vmem,
            scratch_shapes=[
                pltpu.VMEM((z.members, z.variables, z.tiles, ROWS, LANES), f32),
                pltpu.VMEM((z.variables, z.tiles, ROWS, LANES), f32),
                field,
                field,
            ],
            name="descend",
        )(coupling, error_weight, got)
        home = lax.all_to_all(back, axes, 0, 0)
        return pl.pallas_call(
            lambda *refs: unpack_kernel(z, *refs),
            out_shape=(
                jax.ShapeDtypeStruct(weights.shape, f32),
                jax.ShapeDtypeStruct((1, z.variables, ROWS, LANES), f32),
            ),
            in_specs=[vmem],
            out_specs=(vmem, vmem),
            name="unpack",
        )(home)

    return jax.shard_map(
        local,
        mesh=mesh,
        in_specs=(
            P("mem", None, "lat", None),
            P("win", "mem", "lat", None),
            P(None, "lat", "mem"),
            P(),
            P("win"),
            P(("mem", "lat")),
            P(("mem", "lat")),
            P(("mem", "lat")),
            P(("mem", "lat")),
            P(),
        ),
        out_specs=(P("win", "mem", "lat", None), P("win", None, "lat", "mem")),
        check_vma=False,
    )
```

time: 231 us -> 57.1 us (0.25)
  starting transfers between devices: 78.6 us -> 0 us
  waiting for transfers between devices: 78.1 us -> 0 us
  blocking collectives: 17.9 us -> 42.6 us
  local copies, waits for them, and re-layouts: 18.9 us -> 0 us
  other arithmetic: 15 us -> 0 us
  between operations: 15.7 us -> 1.28 us
  Pallas kernels: 0 us -> 12.6 us
  matrix products: 5.13 us -> 0 us
    ppermute x30 -> x0, starting transfers between devices: 78.6 us -> none  [the longest x13 56.7 us: with_halo(): before = lax.ppermute(last, axis, up)]
    reduce_scatter x2 -> x0, waiting for transfers between devices: 52.1 us -> none  [local(): lax.psum_scatter(partial_sum, 'mem', scatter_dimension=2, tiled=True)]
    all_to_all x0 -> x2, blocking collectives: none -> 42.6 us  [the longest x1 29.3 us: local(): got = lax.all_to_all(sent, axes, 0, 0)]
    ppermute x30 -> x0, waiting for transfers between devices: 26 us -> none  [the longest x13 16.8 us: with_halo(): after = lax.ppermute(initial, axis, down)]
    all_gather x2 -> x0, blocking collectives: 17.9 us -> none  [local(): whole_gradient = lax.all_gather(gradient, 'mem', axis=2, tiled=True)]
    pallas_call x0 -> x3, Pallas kernels: none -> 12.6 us  [the longest x1 8.11 us: local(): pl.pallas_call(lambda *refs: descend_kernel(z, scale, *refs), out_shape=j...]
    gather x2 -> x0, local copies, waits for them, and re-layouts: 12.3 us -> none  [local(): picked = flat_state[obs_cell]]
    scatter-add x2 -> x0, other arithmetic: 11.9 us -> none  [local(): jnp.zeros_like(flat_state).at[obs_cell].add(innovation).reshape(ends.shape)]
  transfers between devices with their start and end apart: 32 -> 0, of which waited for: 16 -> 0; matrix products, arithmetic and copies ran while one was open for 13% -> 0% of each run, Pallas kernels for 0% -> 0%
where the time goes in v1:
time: 57.1 us; the launch traced here: 56.5 us
  blocking collectives  42.6 us (75%)
  Pallas kernels  12.6 us (22%)
  between operations  1.28 us (2%)
    all_to_all x1, blocking collectives, local(): got = lax.all_to_all(sent, axes, 0, 0)  29.3 us
    all_to_all x1, blocking collectives, local(): home = lax.all_to_all(back, axes, 0, 0)  13.3 us
    pallas_call x1, Pallas kernels, local(): pl.pallas_call(lambda *refs: descend_kernel(z, scale, *refs), out_shape=j...  8.11 us
    pallas_call x1, Pallas kernels, local(): pl.pallas_call(lambda *refs: pack_kernel(z, *refs), out_shape=jax.ShapeDt...  2.78 us
    pallas_call x1, Pallas kernels, local(): pl.pallas_call(lambda *refs: unpack_kernel(z, *refs), out_shape=(jax.Shap...  1.75 us

profile of v1, /device:TPU:0, one launch (start us, length us, event | category | flops | bytes accessed | tf_op | source)
XLA Modules:
  0.0 56.5 jit_solution(16379983583275488064)
XLA Ops:
  1.3 2.8 %pack.1 = f32[32,48,128]{2,1,0:T(8,128)} custom-call(s32[1]{0:T(128)S(6)} %copy.12.refs_0_, f32[2,8,8,512]{3,2,1,0:T(8,128)} %refs_1_.2, f32[1,2,8,512]{3,2,1,0:T(8,128)} %refs_2_.1, f32[8,8,128]{2,1,0:T(8,128)} %refs_3_.1, s32[8,128]{1,0:T(8,128)} %bitcast.4, s32[8,128]{1,0:T(8,128)} %bitcast.5, f32[8,128]{1,0:T(8,128)} %bitcast.6, f32[8,128]{1,0:T(8,128)} %bitcast.7), custom_call_target="tpu_custom_call" | custom-call | tf_op jit(solution)/shard_map/pack/pallas_call | solution.py:381
  4.1 29.3 %all_to_all.10.refs_2_ = f32[32,48,128]{2,1,0:T(8,128)} all-to-all(f32[32,48,128]{2,1,0:T(8,128)} %pack.1), channel_id=1, replica_groups=mesh['mem'=4,'lat'=4,'win'=2] {'mem','lat','win'}, dimensions={0} | all-to-all | bytes 1572864 | tf_op jit(solution)/shard_map/all_to_all | solution.py:389
  33.3 8.1 %descend.1 = f32[32,16,128]{2,1,0:T(8,128)} custom-call(f32[8,8]{1,0:T(8,128)} %refs_0_.2, f32[8]{0:T(128)} %refs_1_.3, f32[32,48,128]{2,1,0:T(8,128)} %all_to_all.10.refs_2_), custom_call_target="tpu_custom_call" | custom-call | tf_op jit(solution)/shard_map/descend/pallas_call | solution.py:391
  41.5 13.3 %all_to_all.11.refs_0_ = f32[32,16,128]{2,1,0:T(8,128)} all-to-all(f32[32,16,128]{2,1,0:T(8,128)} %descend.1), channel_id=1, replica_groups=mesh['mem'=4,'lat'=4,'win'=2] {'mem','lat','win'}, dimensions={0} | all-to-all | bytes 524288 | tf_op jit(solution)/shard_map/all_to_all | solution.py:404
  54.7 1.8 %unpack.1 = (f32[1,2,8,512]{3,2,1,0:T(8,128)}, f32[1,8,8,128]{3,2,1,0:T(8,128)}) custom-call(f32[32,16,128]{2,1,0:T(8,128)} %all_to_all.11.refs_0_), custom_call_target="tpu_custom_call" | custom-call | tf_op jit(solution)/shard_map/unpack/pallas_call | solution.py:405

commit v2 on v1

--- a/solution.py
+++ b/solution.py
@@ -80,19 +80,39 @@
         assert obs_here % (self.win * LANES) == 0
 
 
-def pack_kernel(z, steps, ens, wts, dif, cell, window, value, weight, out, obs):
+def pack_kernel(z, steps, ens_hbm, wts_hbm, dif_hbm, cell_hbm, window_hbm, value_hbm, weight_hbm, out, *scratch):
+    ens, wts, dif, cell, window, value, weight, obs, sems = scratch
     k = lax.axis_index("win")
-    units = [ens[m, k * z.vars_here + v] for m in range(z.members_here) for v in range(z.vars_here)]
-    for reg in range(z.ens_regs):
-        for d, part in windows(units[reg * GROUPS : (reg + 1) * GROUPS], z.own):
-            out[d, reg * ROWS : (reg + 1) * ROWS, :] = part
+    mine = pl.ds(k * z.vars_here, z.vars_here)
+    copies = [
+        pltpu.make_async_copy(source, target, sems.at[n])
+        for n, (source, target) in enumerate([
+            (dif_hbm.at[mine], dif),
+            (ens_hbm.at[:, mine], ens),
+            (cell_hbm, cell),
+            (window_hbm, window),
+            (value_hbm, value),
+            (weight_hbm, weight),
+            (wts_hbm, wts),
+        ])
+    ]
+    for copy in copies:
+        copy.start()
+    copies[0].wait()
     per_block = LANES // z.own
     for reg in range(z.dif_regs):
         mine = range(reg * GROUPS, min(z.vars_here, (reg + 1) * GROUPS))
         at = z.dif_at + reg * ROWS
-        for d, part in windows([dif[k * z.vars_here + v] for v in mine], z.own):
+        for d, part in windows([dif[v] for v in mine], z.own):
             for block in range(z.mem):
                 out[block * per_block + d, at : at + ROWS, :] = part
+    copies[1].wait()
+    units = [ens[m, v] for m in range(z.members_here) for v in range(z.vars_here)]
+    for reg in range(z.ens_regs):
+        for d, part in windows(units[reg * GROUPS : (reg + 1) * GROUPS], z.own):
+            out[d, reg * ROWS : (reg + 1) * ROWS, :] = part
+    for copy in copies[2:]:
+        copy.wait()
     count = jnp.full((ROWS, LANES), steps[0], jnp.int32).astype(jnp.float32)
     holds_weights = lane_ids() // SPAN < z.members_here
     for d, part in windows([wts[0, m] for m in range(z.members_here)], z.own):
@@ -371,6 +391,8 @@
 def solution(mesh):
     smem = pl.BlockSpec(memory_space=pltpu.SMEM)
     vmem = pl.BlockSpec(memory_space=pltpu.VMEM)
+    hbm = pl.BlockSpec(memory_space=pltpu.HBM)
+    limit = 24 << 20
     f32 = jnp.float32
 
     def local(ensemble, weights, diffusivity, coupling, tl_steps, obs_cell, obs_window, obs_value, obs_weight, error_weight):
@@ -381,11 +403,19 @@
         sent = pl.pallas_call(
             lambda *refs: pack_kernel(z, *refs),
             out_shape=jax.ShapeDtypeStruct((z.devices, z.chunk, LANES), f32),
-            in_specs=[smem] + [vmem] * 7,
+            in_specs=[smem] + [hbm] * 7,
             out_specs=vmem,
-            scratch_shapes=[pltpu.VMEM((ROWS * z.obs_regs, LANES), f32)],
+            scratch_shapes=[
+                pltpu.VMEM((z.members_here, z.vars_here, ROWS, z.lon), f32),
+                pltpu.VMEM(weights.shape, f32),
+                pltpu.VMEM((z.vars_here, ROWS, LANES), f32),
+                *(pltpu.VMEM(x.shape, x.dtype) for x in tables),
+                pltpu.VMEM((ROWS * z.obs_regs, LANES), f32),
+                pltpu.SemaphoreType.DMA((7,)),
+            ],
+            compiler_params=pltpu.CompilerParams(vmem_limit_bytes=limit),
             name="pack",
-        )(tl_steps, ensemble, weights, diffusivity, *tables)
+        )(tl_steps, *(pltpu.with_memory_space_constraint(x, pltpu.HBM) for x in (ensemble, weights, diffusivity, *tables)))
         got = lax.all_to_all(sent, axes, 0, 0)
         field = pltpu.VMEM((z.pairs, z.variables, z.tiles, ROWS, LANES), f32)
         back = pl.pallas_call(
@@ -399,6 +429,7 @@
                 field,
                 field,
             ],
+            compiler_params=pltpu.CompilerParams(vmem_limit_bytes=limit),
             name="descend",
         )(coupling, error_weight, got)
         home = lax.all_to_all(back, axes, 0, 0)
@@ -410,6 +441,7 @@
             ),
             in_specs=[vmem],
             out_specs=(vmem, vmem),
+            compiler_params=pltpu.CompilerParams(vmem_limit_bytes=limit),
             name="unpack",
         )(home)
 

time: 57.1 us -> 51.5 us (0.902)
  Pallas kernels: 12.6 us -> 8.51 us
  blocking collectives: 42.6 us -> 41.1 us
    pallas_call x1, Pallas kernels: 8.11 us -> 6.08 us  [local(): pl.pallas_call(lambda *refs: descend_kernel(z, scale, *refs), out_shape=j...]
    all_to_all x1, blocking collectives: 13.3 us -> 12.1 us  [local(): home = lax.all_to_all(back, axes, 0, 0)]
    pallas_call x1, Pallas kernels: 2.78 us -> 1.63 us  [local(): pl.pallas_call(lambda *refs: pack_kernel(z, *refs), out_shape=jax.ShapeDt...]
    pallas_call x1, Pallas kernels: 1.75 us -> 0.8 us  [local(): pl.pallas_call(lambda *refs: unpack_kernel(z, *refs), out_shape=(jax.Shap...]
where the time goes in v2:
time: 51.5 us; the launch traced here: 50.9 us
  blocking collectives  41.1 us (80%)
  Pallas kernels  8.51 us (17%)
  between operations  1.31 us (3%)
    all_to_all x1, blocking collectives, local(): got = lax.all_to_all(sent, axes, 0, 0)  29 us
    all_to_all x1, blocking collectives, local(): home = lax.all_to_all(back, axes, 0, 0)  12.1 us
    pallas_call x1, Pallas kernels, local(): pl.pallas_call(lambda *refs: descend_kernel(z, scale, *refs), out_shape=j...  6.08 us
    pallas_call x1, Pallas kernels, local(): pl.pallas_call(lambda *refs: pack_kernel(z, *refs), out_shape=jax.ShapeDt...  1.63 us

profile of v2, /device:TPU:0, one launch (start us, length us, event | category | flops | bytes accessed | tf_op | source)
XLA Modules:
  0.0 50.9 jit_solution(6871269897402745827)
XLA Ops:
  1.3 1.6 %pack.1 = f32[32,48,128]{2,1,0:T(8,128)S(1)} custom-call(s32[1]{0:T(128)S(6)} %copy.12.refs_0_, f32[2,8,8,512]{3,2,1,0:T(8,128)} %refs_1_.2, f32[1,2,8,512]{3,2,1,0:T(8,128)} %refs_2_.1, f32[8,8,128]{2,1,0:T(8,128)} %refs_3_.1, s32[8,128]{1,0:T(8,128)} %bitcast.4, s32[8,128]{1,0:T(8,128)} %bitcast.5, f32[8,128]{1,0:T(8,128)} %bitcast.6, f32[8,128]{1,0:T(8,128)} %bitcast.7), custom_call_target="tpu_custom_call" | custom-call | tf_op jit(solution)/shard_map/pack/pallas_call | solution.py:403
  2.9 0.0 copy-start
  2.9 0.0 copy-start.1
  2.9 29.0 %all_to_all.10.refs_2_ = f32[32,48,128]{2,1,0:T(8,128)S(1)} all-to-all(f32[32,48,128]{2,1,0:T(8,128)S(1)} %pack.1), channel_id=1, replica_groups=mesh['mem'=4,'lat'=4,'win'=2] {'mem','lat','win'}, dimensions={0} | all-to-all | bytes 1572864 | tf_op jit(solution)/shard_map/all_to_all | solution.py:419
  31.9 0.0 copy-done
  31.9 0.0 copy-done.1
  31.9 6.1 %descend.1 = f32[32,16,128]{2,1,0:T(8,128)S(1)} custom-call(f32[8,8]{1,0:T(8,128)S(1)} %copy-done, f32[8]{0:T(128)S(1)} %copy-done.1, f32[32,48,128]{2,1,0:T(8,128)S(1)} %all_to_all.10.refs_2_), custom_call_target="tpu_custom_call" | custom-call | tf_op jit(solution)/shard_map/descend/pallas_call | solution.py:421
  38.0 12.1 %all_to_all.11.refs_0_ = f32[32,16,128]{2,1,0:T(8,128)S(1)} all-to-all(f32[32,16,128]{2,1,0:T(8,128)S(1)} %descend.1), channel_id=1, replica_groups=mesh['mem'=4,'lat'=4,'win'=2] {'mem','lat','win'}, dimensions={0} | all-to-all | bytes 524288 | tf_op jit(solution)/shard_map/all_to_all | solution.py:435
  50.1 0.8 %unpack.1 = (f32[1,2,8,512]{3,2,1,0:T(8,128)}, f32[1,8,8,128]{3,2,1,0:T(8,128)}) custom-call(f32[32,16,128]{2,1,0:T(8,128)S(1)} %all_to_all.11.refs_0_), custom_call_target="tpu_custom_call" | custom-call | tf_op jit(solution)/shard_map/unpack/pallas_call | solution.py:436
Async XLA Ops:
  2.9 29.0 %copy-start = (f32[8,8]{1,0:T(8,128)S(1)}, f32[8,8]{1,0:T(8,128)}, u32[]{:S(2)}) copy-start(f32[8,8]{1,0:T(8,128)} %refs_0_.2) | copy-start | bytes 772
  2.9 29.0 %copy-start.1 = (f32[8]{0:T(128)S(1)}, f32[8]{0:T(128)}, u32[]{:S(2)}) copy-start(f32[8]{0:T(128)} %refs_1_.3) | copy-start | bytes 100

commit v3 on v1

v3 whole, which is shorter than its diff:
```python
import math

import jax
import jax.numpy as jnp
from jax import lax
from jax.experimental import pallas as pl
from jax.experimental.pallas import tpu as pltpu
from jax.sharding import PartitionSpec as P

KMAX = 6
DIFF = 2
ITERS = 2
KAPPA = 0.125
DESCENT = 0.25

ROWS = 8
LANES = 128
SPAN = 32
GROUPS = LANES // SPAN
HALF = ROWS // 2
PAIR = ROWS // GROUPS


def roll(x, shift, axis):
    shift %= x.shape[axis]
    return x if shift == 0 else pltpu.roll(x, shift, axis)


def lane_ids():
    return lax.broadcasted_iota(jnp.int32, (ROWS, LANES), 1)


def pad4(units):
    return list(units) + [jnp.zeros_like(units[0])] * (GROUPS - len(units))


def exchange4(x):
    group = lane_ids() // SPAN
    low, even = group < 2, group % 2 == 0
    a = [jnp.where(low, x[u], roll(x[u + 2], 64, 1)) for u in range(2)]
    b = [jnp.where(low, roll(x[u], 64, 1), x[u + 2]) for u in range(2)]
    out = []
    for first, second in (a, b):
        out.append(jnp.where(even, first, roll(second, SPAN, 1)))
        out.append(jnp.where(even, roll(first, -SPAN, 1), second))
    return out


def windows(units, own):
    halo, phases, length = (SPAN - own) // 2, SPAN // own, units[0].shape[1]
    for phase in range(phases):
        moved = pad4([roll(u, halo - own * phase, 1) for u in units])
        for tile in range(length // LANES):
            parts = exchange4([m[:, tile * LANES : (tile + 1) * LANES] for m in moved])
            for q, part in enumerate(parts):
                yield (tile * GROUPS + q) * phases + phase, part


class Sizes:
    def __init__(self, mesh_shape, members_here, variables, lon, obs_here):
        self.mem, self.lat, self.win = (mesh_shape[a] for a in ("mem", "lat", "win"))
        self.devices = self.mem * self.lat * self.win
        self.members_here, self.variables, self.lon = members_here, variables, lon
        self.members = members_here * self.mem
        self.vars_here = variables // self.win
        self.own = lon // self.devices
        self.halo = (SPAN - self.own) // 2
        self.tiles = self.lat // 2
        self.pairs = self.win // 2
        self.obs_rows = obs_here // self.win // LANES
        self.ens_regs = pl.cdiv(members_here * self.vars_here, GROUPS)
        self.dif_regs = pl.cdiv(self.vars_here, GROUPS)
        self.dif_at = ROWS * self.ens_regs
        self.wts_at = self.dif_at + ROWS * self.dif_regs
        self.obs_at = self.wts_at + HALF
        self.chunk = self.obs_at + 4 * self.obs_rows
        self.back = PAIR + ROWS
        assert lon // self.mem == LANES and members_here * SPAN <= LANES // 2 and members_here * self.own <= SPAN
        assert self.chunk % HALF == 0
        assert self.halo >= 2 * DIFF * ITERS
        assert self.lat % 2 == 0 and self.win % 2 == 0 and variables % self.win == 0
        assert SPAN % self.own == 0 and variables * self.own <= LANES
        assert obs_here % (self.win * LANES) == 0


def pack_kernel(z, steps, *refs):
    sources, (out, coup, error), scratch, sems = refs[:9], refs[9:12], refs[12:21], refs[21]
    coupling_in, error_in, dif, ens, cell, window, value, weight, wts = scratch
    k = lax.axis_index("win")
    mine = pl.ds(k * z.vars_here, z.vars_here)
    copies = []
    for n, (source, target) in enumerate(zip(sources, scratch)):
        source = source.at[mine] if target is dif else source.at[:, mine] if target is ens else source
        copies.append(pltpu.make_async_copy(source, target, sems.at[n]))
        copies[-1].start()
    copies[0].wait()
    copies[1].wait()
    for v in range(z.variables):
        error[v] = jnp.broadcast_to(error_in[:, v : v + 1], (ROWS, LANES))
        for w in range(z.variables):
            coup[v, w] = jnp.broadcast_to(coupling_in[v : v + 1, w : w + 1], (ROWS, LANES))
    copies[2].wait()
    per_block = LANES // z.own
    count = jnp.full((ROWS, LANES), steps[0], jnp.int32).astype(jnp.float32)
    spare = lane_ids() % SPAN == 0
    for reg in range(z.dif_regs):
        mine = range(reg * GROUPS, min(z.vars_here, (reg + 1) * GROUPS))
        for d, part in windows([dif[v] for v in mine], z.own):
            part = jnp.where(spare, count, part)
            for block in range(z.mem):
                at = (block * per_block + d) * z.chunk + z.dif_at + reg * ROWS
                out[at : at + ROWS, :] = part
    copies[3].wait()
    units = [ens[m, v] for m in range(z.members_here) for v in range(z.vars_here)]
    for reg in range(z.ens_regs):
        for d, part in windows(units[reg * GROUPS : (reg + 1) * GROUPS], z.own):
            at = d * z.chunk + reg * ROWS
            out[at : at + ROWS, :] = part
    for copy in copies[4:]:
        copy.wait()
    low = lane_ids() < LANES // 2
    for d, part in windows([wts[0, m] for m in range(z.members_here)], z.own):
        at = d * z.chunk + z.wts_at
        out[at : at + HALF, :] = jnp.where(low, part, roll(roll(part, LANES // 2, 1), HALF, 0))[:HALF]
    n = z.obs_rows
    for a, ref in enumerate((cell, window, value, weight)):
        rows = ref[0:n, :]
        for other in range(1, z.win):
            rows = jnp.where(k == other, ref[other * n : (other + 1) * n, :], rows)
        rows = rows.astype(jnp.float32)
        for d in range(z.devices):
            at = d * z.chunk + z.obs_at + a * n
            out[at : at + n, :] = rows


def spread4(first, second):
    group = lane_ids() // SPAN
    low, even = group < 2, group % 2 == 0
    a = jnp.where(even, first, roll(second, SPAN, 1))
    b = jnp.where(even, roll(first, -SPAN, 1), second)
    a2, b2 = roll(a, 64, 1), roll(b, 64, 1)
    return [jnp.where(low, a, a2), jnp.where(low, b, b2), jnp.where(low, a2, a), jnp.where(low, b2, b)]


def place(pieces, width):
    target = lax.broadcasted_iota(jnp.int32, pieces[0][0].shape, 1) // width
    out = None
    for g, (x, lane) in enumerate(pieces):
        moved = roll(x, width * g - lane, 1)
        out = moved if out is None else jnp.where(target == g, moved, out)
    return out


def split(x):
    high = x.astype(jnp.bfloat16).astype(jnp.float32)
    return high, x - high


def descend_kernel(z, scale, coup, error_weight, recv, out, ens, dif, own, slope, bias):
    i, j, k = (lax.axis_index(a) for a in ("mem", "lat", "win"))
    d = (i * z.lat + j) * z.win + k
    start = lax.rem(d * z.own - z.halo + z.lon, z.lon)
    left = lax.div(start, LANES)
    right = lax.div(lax.rem(start + SPAN - 1, z.lon), LANES)
    lanes = lane_ids()
    sub = lax.broadcasted_iota(jnp.int32, (ROWS, LANES), 0)
    group = lanes // SPAN
    upper = group % 2 == 0
    in_left = start + lanes % SPAN < (left + 1) * LANES
    T, NV, M = z.tiles, z.variables, z.members

    def source(mem, lat, win):
        return (mem * z.lat + lat) * z.win + win

    def take(mem, lat, win, at, rows):
        first = source(mem, lat, win) * z.chunk
        return recv[pl.ds((first if isinstance(first, int) else pl.multiple_of(first, HALF)) + at, rows), :]

    for mem in range(z.mem):
        for win in range(z.win):
            for reg in range(z.ens_regs):
                for t in range(T):
                    got = spread4(*(take(mem, h * T + t, win, reg * ROWS, ROWS) for h in range(2)))
                    for u, part in enumerate(got):
                        unit = reg * GROUPS + u
                        if unit < z.members_here * z.vars_here:
                            m = mem * z.members_here + unit // z.vars_here
                            v = win * z.vars_here + unit % z.vars_here
                            ens[m, v, t] = part
    for win in range(z.win):
        for reg in range(z.dif_regs):
            at = z.dif_at + reg * ROWS
            for t in range(T):
                both = [
                    jnp.where(in_left, take(left, h * T + t, win, at, ROWS), take(right, h * T + t, win, at, ROWS))
                    for h in range(2)
                ]
                for u, part in enumerate(spread4(*both)):
                    if reg * GROUPS + u < z.vars_here:
                        dif[win * z.vars_here + reg * GROUPS + u, t] = jnp.where(lanes % SPAN == 0, 0.0, part)

    def weights_of(mem, lat, win):
        x = take(mem, lat, win, z.wts_at, HALF)
        return jnp.concatenate([x, roll(x, LANES // 2, 1)], 0)

    control = [[[None] * T for _ in range(z.pairs)] for _ in range(M)]
    for mem in range(z.mem):
        for p in range(z.pairs):
            for t in range(T):
                quarter = [weights_of(mem, h * T + t, 2 * p + w) for w in range(2) for h in range(2)]
                for unit in range(z.members_here):
                    control[mem * z.members_here + unit][p][t] = place([(x, SPAN * unit) for x in quarter], SPAN)
    steps = [jnp.broadcast_to(take(0, 0, win, z.dif_at, 1)[:, :1], (ROWS, LANES)) for win in range(z.win)]
    counts = [jnp.where(group < 2, steps[2 * p], steps[2 * p + 1]).astype(jnp.int32) for p in range(z.pairs)]

    bf16 = jnp.bfloat16
    row_id = lax.broadcasted_iota(jnp.int32, (z.win * NV * ROWS, LANES), 0).astype(jnp.float32).astype(bf16)
    lane_id = lax.broadcasted_iota(jnp.int32, (SPAN, LANES), 0).astype(jnp.float32).astype(bf16)
    one, none = jnp.ones((), bf16), jnp.zeros((), bf16)
    n = z.obs_rows

    def column(x, like):
        return jnp.broadcast_to(x, like.shape).astype(bf16)

    for lat in range(z.lat):
        hot, parts = [], []
        for side, block in enumerate((left, right)):
            for win in range(z.win):
                where, time, value, weight = (take(block, lat, win, z.obs_at + a * n, n) for a in range(4))
                where = where.astype(jnp.int32)
                weighted = weight * value
                lane = block * LANES + where % LANES - start
                lane = jnp.where(lane < 0, lane + z.lon, lane)
                inside = lane < SPAN
                if side == 1:
                    inside &= left != right
                lane = jnp.where(inside, lane, -1).astype(jnp.float32)
                row = time * (NV * ROWS) + (where // LANES).astype(jnp.float32)
                values = [x for pair in zip(split(weight), split(weighted)) for x in pair]
                for x in range(n):
                    at = slice(x, x + 1)
                    hit = column(lane[at], lane_id) == lane_id
                    hot.append(jnp.where(column(row[at], row_id) == row_id, one, none))
                    parts.append(jnp.concatenate([jnp.where(hit, column(y[at], lane_id), none) for y in values], 0))
        total = lax.dot_general(
            jnp.concatenate(hot, 1),
            jnp.concatenate(parts, 1),
            (((1,), (1,)), ((), ())),
            preferred_element_type=jnp.float32,
        )
        h, t = divmod(lat, T)
        for p in range(z.pairs):
            for v in range(NV):
                sums = []
                for w in range(2):
                    at = ((2 * p + w) * NV + v) * ROWS
                    x = total[at : at + ROWS, :]
                    sums.append(x + roll(x, 2 * SPAN, 1))
                both = jnp.where(group < 2, sums[0], sums[1])
                x, y = (both, roll(both, -SPAN, 1)) if h == 0 else (roll(both, SPAN, 1), both)
                if h == 0:
                    slope[p, v, t], bias[p, v, t] = x, y
                else:
                    slope[p, v, t] = jnp.where(upper, slope[p, v, t], x)
                    bias[p, v, t] = jnp.where(upper, bias[p, v, t], y)

    first, last = sub == 0, sub == ROWS - 1

    def beside(x):
        down = [roll(a, 1, 0) for a in x]
        up = [roll(a, -1, 0) for a in x]
        before_first = jnp.where(upper, 0.0, roll(down[T - 1], SPAN, 1))
        after_last = jnp.where(upper, roll(up[0], -SPAN, 1), 0.0)
        return [
            jnp.where(first, down[t - 1] if t else before_first, down[t])
            + jnp.where(last, up[t + 1] if t < T - 1 else after_last, up[t])
            for t in range(T)
        ]

    def smooth(x):
        for _ in range(DIFF):
            x = [
                (1.0 - 4.0 * KAPPA) * a + KAPPA * (rows + roll(a, 1, 1) + roll(a, -1, 1))
                for a, rows in zip(x, beside(x))
            ]
        return x

    def weigh(terms):
        total = None
        for factor, x in terms:
            total = factor * x if total is None else total + factor * x
        return total

    for v in range(NV):
        for t in range(T):
            own[v, t] = 1.0 - 2.0 * dif[v, t] + coup[v, v]

    def repeat(step, state, p):
        def section(index, flat):
            moved = step([list(flat[v * T : (v + 1) * T]) for v in range(NV)])
            on = index < counts[p]
            return tuple(jnp.where(on, x, y) for x, y in zip((x for v in moved for x in v), flat))

        flat = lax.fori_loop(0, most[p], section, tuple(x for v in state for x in v))
        return [list(flat[v * T : (v + 1) * T]) for v in range(NV)]

    def forward(u):
        moved = []
        for v in range(NV):
            near = beside(u[v])
            moved.append([
                own[v, t] * u[v][t] + dif[v, t] * near[t] + weigh((coup[v, w], u[w][t]) for w in range(NV) if w != v)
                for t in range(T)
            ])
        return moved

    def backward(u):
        moved = []
        for v in range(NV):
            near = beside([dif[v, t] * u[v][t] for t in range(T)])
            moved.append([
                own[v, t] * u[v][t] + near[t] + weigh((coup[w, v], u[w][t]) for w in range(NV) if w != v) for t in range(T)
            ])
        return moved

    most = [jnp.max(c) for c in counts]
    later = group >= 2
    zero = jnp.zeros((ROWS, LANES), jnp.float32)
    for _ in range(ITERS):
        increment, ends = [], []
        smoothed = [[smooth(control[m][p]) for p in range(z.pairs)] for m in range(M)]
        for p in range(z.pairs):
            increment.append(
                [[weigh((ens[m, v, t], smoothed[m][p][t]) for m in range(M)) * scale for t in range(T)] for v in range(NV)]
            )
            ends.append(repeat(forward, increment[p], p))
        misfit = []
        for p in range(z.pairs):
            misfit.append([])
            for v in range(NV):
                misfit[p].append([])
                for t in range(T):
                    before = roll(ends[p][v][t], 64, 1)
                    if p:
                        before = jnp.where(later, before, roll(ends[p - 1][v][t], 64, 1))
                    x = error_weight[v] * (before - increment[p][v][t])
                    misfit[p][v].append(x if p else jnp.where(later, x, 0.0))
        members_back = [[] for _ in range(M)]
        for p in range(z.pairs):
            forcing = []
            for v in range(NV):
                forcing.append([])
                for t in range(T):
                    after = roll(misfit[p + 1][v][t], 64, 1) if p + 1 < z.pairs else zero
                    after = jnp.where(later, after, roll(misfit[p][v][t], 64, 1))
                    forcing[v].append(slope[p, v, t] * ends[p][v][t] - bias[p, v, t] + after)
            adjoint = repeat(backward, forcing, p)
            gradient = [[adjoint[v][t] - misfit[p][v][t] for t in range(T)] for v in range(NV)]
            for m in range(M):
                members_back[m].append(
                    [weigh((ens[m, v, t], gradient[v][t]) for v in range(NV)) * scale for t in range(T)]
                )
        for m in range(M):
            for p in range(z.pairs):
                pulled = smooth(members_back[m][p])
                control[m][p] = [c - DESCENT * (c + x) for c, x in zip(control[m][p], pulled)]

    for lat in range(z.lat):
        h, t = divmod(lat, T)
        for win in range(z.win):
            p, w = divmod(win, 2)
            lane = SPAN * (2 * w + h) + z.halo
            grown = place([(increment[p][v][t], lane) for v in range(NV)], z.own)
            for mem in range(z.mem):
                to = source(mem, lat, win)
                mine = [control[mem * z.members_here + m][p][t] for m in range(z.members_here)]
                x = place([(x, lane) for x in mine], z.own)
                folded = place([(roll(x, -PAIR * q, 0), 0) for q in range(GROUPS)], SPAN)
                out[to * z.back : to * z.back + PAIR, :] = folded[:PAIR]
                out[to * z.back + PAIR : (to + 1) * z.back, :] = grown


def unpack_kernel(z, recv, control, increment):
    per_tile = LANES // z.own
    for tile in range(z.lon // LANES):
        got = [recv[d * z.back : d * z.back + PAIR, :] for d in range(tile * per_tile, (tile + 1) * per_tile)]
        for m in range(z.members_here):
            for q in range(GROUPS):
                control[0, m, PAIR * q : PAIR * (q + 1), tile * LANES : (tile + 1) * LANES] = place(
                    [(x, SPAN * q + z.own * m) for x in got], z.own
                )
    first = lax.axis_index("mem") * per_tile
    got = [recv[pl.ds(pl.multiple_of((first + q) * z.back, PAIR) + PAIR, ROWS), :] for q in range(per_tile)]
    for v in range(z.variables):
        increment[0, v] = place([(x, z.own * v) for x in got], z.own)


def in_hbm(*arrays):
    return [pltpu.with_memory_space_constraint(x, pltpu.HBM) for x in arrays]


def solution(mesh):
    smem = pl.BlockSpec(memory_space=pltpu.SMEM)
    vmem = pl.BlockSpec(memory_space=pltpu.VMEM)
    hbm = pl.BlockSpec(memory_space=pltpu.HBM)
    f32 = jnp.float32

    def local(ensemble, weights, diffusivity, coupling, tl_steps, obs_cell, obs_window, obs_value, obs_weight, error_weight):
        z = Sizes(mesh.shape, ensemble.shape[0], ensemble.shape[1], ensemble.shape[3], obs_cell.shape[0])
        scale = 1.0 / math.sqrt(z.members - 1)
        tables = [x.reshape(-1, LANES) for x in (obs_cell, obs_window, obs_value, obs_weight)]
        params = pltpu.CompilerParams(vmem_limit_bytes=24 << 20)
        reg = (ROWS, LANES)
        field = pltpu.VMEM((z.pairs, z.variables, z.tiles, *reg), f32)
        still = pltpu.VMEM((z.variables, z.tiles, *reg), f32)

        def exchange(x, rows):
            step = math.gcd(rows, ROWS)
            split = x.reshape(z.devices, rows // step, step, LANES)
            return lax.all_to_all(split, ("mem", "lat", "win"), 0, 0).reshape(x.shape)

        sent, coup, error = pl.pallas_call(
            lambda *refs: pack_kernel(z, *refs),
            out_shape=(
                jax.ShapeDtypeStruct((z.devices * z.chunk, LANES), f32),
                jax.ShapeDtypeStruct((z.variables, z.variables, *reg), f32),
                jax.ShapeDtypeStruct((z.variables, *reg), f32),
            ),
            in_specs=[smem] + [hbm] * 9,
            out_specs=(vmem, vmem, vmem),
            scratch_shapes=[
                pltpu.VMEM(coupling.shape, f32),
                pltpu.VMEM((1, z.variables), f32),
                pltpu.VMEM((z.vars_here, *reg), f32),
                pltpu.VMEM((z.members_here, z.vars_here, ROWS, z.lon), f32),
                *(pltpu.VMEM(x.shape, x.dtype) for x in tables),
                pltpu.VMEM(weights.shape, f32),
                pltpu.SemaphoreType.DMA((9,)),
            ],
            compiler_params=params,
            name="pack",
        )(tl_steps, *in_hbm(coupling, error_weight.reshape(1, -1), diffusivity, ensemble, *tables, weights))
        back = pl.pallas_call(
            lambda *refs: descend_kernel(z, scale, *refs),
            out_shape=jax.ShapeDtypeStruct((z.devices * z.back, LANES), f32),
            in_specs=[vmem, vmem, vmem],
            out_specs=vmem,
            scratch_shapes=[
                pltpu.VMEM((z.members, z.variables, z.tiles, *reg), f32),
                still,
                still,
                field,
                field,
            ],
            compiler_params=params,
            name="descend",
        )(coup, error, exchange(sent, z.chunk))
        home = exchange(back, z.back)
        return pl.pallas_call(
            lambda *refs: unpack_kernel(z, *refs),
            out_shape=(
                jax.ShapeDtypeStruct(weights.shape, f32),
                jax.ShapeDtypeStruct((1, z.variables, ROWS, LANES), f32),
            ),
            in_specs=[vmem],
            out_specs=(vmem, vmem),
            compiler_params=params,
            name="unpack",
        )(home)

    return jax.shard_map(
        local,
        mesh=mesh,
        in_specs=(
            P("mem", None, "lat", None),
            P("win", "mem", "lat", None),
            P(None, "lat", "mem"),
            P(),
            P("win"),
            P(("mem", "lat")),
            P(("mem", "lat")),
            P(("mem", "lat")),
            P(("mem", "lat")),
            P(),
        ),
        out_specs=(P("win", "mem", "lat", None), P("win", None, "lat", "mem")),
        check_vma=False,
    )
```

time: 57.1 us -> 49.3 us (0.86)
  blocking collectives: 42.6 us -> 38.2 us
  Pallas kernels: 12.6 us -> 9.51 us
    all_to_all x2, blocking collectives: 42.6 us -> 38.2 us  [exchange(): return lax.all_to_all(split, ('mem', 'lat', 'win'), 0, 0).reshape(x.shape)]
    pallas_call x1, Pallas kernels: 8.11 us -> 6.67 us  [local(): pl.pallas_call(lambda *refs: descend_kernel(z, scale, *refs), out_shape=j...]
    pallas_call x1, Pallas kernels: 2.78 us -> 1.86 us  [local(): pl.pallas_call(lambda *refs: pack_kernel(z, *refs), out_shape=(jax.ShapeD...]
    pallas_call x1, Pallas kernels: 1.75 us -> 0.98 us  [local(): pl.pallas_call(lambda *refs: unpack_kernel(z, *refs), out_shape=(jax.Shap...]
where the time goes in v3:
time: 49.3 us; the launch traced here: 49 us
  blocking collectives  38.2 us (77%)
  Pallas kernels  9.51 us (19%)
  between operations  1.3 us (3%)
    all_to_all x2, blocking collectives, exchange(): return lax.all_to_all(split, ('mem', 'lat', 'win'), 0, 0).reshape(x.shape)  38.2 us
    pallas_call x1, Pallas kernels, local(): pl.pallas_call(lambda *refs: descend_kernel(z, scale, *refs), out_shape=j...  6.67 us
    pallas_call x1, Pallas kernels, local(): pl.pallas_call(lambda *refs: pack_kernel(z, *refs), out_shape=(jax.ShapeD...  1.86 us

profile of v3, /device:TPU:0, one launch (start us, length us, event | category | flops | bytes accessed | tf_op | source)
XLA Modules:
  0.0 49.0 jit_solution(6426103066730166386)
XLA Ops:
  1.3 1.9 %pack.1 = (f32[1408,128]{1,0:T(8,128)S(1)}, f32[8,8,8,128]{3,2,1,0:T(8,128)S(1)}, f32[8,8,128]{2,1,0:T(8,128)S(1)}) custom-call(s32[1]{0:T(128)S(6)} %copy.12.refs_0_, f32[8,8]{1,0:T(8,128)} %refs_1_.1, f32[1,8]{1,0:T(1,128)} %bitcast.17, f32[8,8,128]{2,1,0:T(8,128)} %refs_3_.1, f32[2,8,8,512]{3,2,1,0:T(8,128)} %refs_4_.1, s32[8,128]{1,0:T(8,128)} %bitcast.13, ...), custom_call_target="tpu_custom_call" | custom-call | tf_op jit(solution)/shard_map/pack/pallas_call | solution.py:422
  3.1 27.6 %all_to_all.10 = f32[32,11,4,128]{3,2,1,0:T(4,128)S(1)} all-to-all(f32[32,11,4,128]{3,2,1,0:T(4,128)S(1)} %bitcast.10), channel_id=1, replica_groups=mesh['mem'=4,'lat'=4,'win'=2] {'mem','lat','win'}, dimensions={0} | all-to-all | bytes 1441792 | tf_op jit(solution)/shard_map/all_to_all | solution.py:420
  30.7 6.7 %descend.1 = f32[320,128]{1,0:T(8,128)S(1)} custom-call(f32[8,8,8,128]{3,2,1,0:T(8,128)S(1)} %get-tuple-element.5.refs_0_, f32[8,8,128]{2,1,0:T(8,128)S(1)} %get-tuple-element.6.refs_1_, f32[1408,128]{1,0:T(8,128)S(1)} %bitcast.9), custom_call_target="tpu_custom_call" | custom-call | tf_op jit(solution)/shard_map/descend/pallas_call | solution.py:443
  37.4 10.6 %all_to_all.11 = f32[32,5,2,128]{3,2,1,0:T(2,128)S(1)} all-to-all(f32[32,5,2,128]{3,2,1,0:T(2,128)S(1)} %bitcast.11), channel_id=1, replica_groups=mesh['mem'=4,'lat'=4,'win'=2] {'mem','lat','win'}, dimensions={0} | all-to-all | bytes 327680 | tf_op jit(solution)/shard_map/all_to_all | solution.py:420
  48.0 1.0 %unpack.1 = (f32[1,2,8,512]{3,2,1,0:T(8,128)}, f32[1,8,8,128]{3,2,1,0:T(8,128)}) custom-call(f32[320,128]{1,0:T(8,128)S(1)} %bitcast.12), custom_call_target="tpu_custom_call" | custom-call | tf_op jit(solution)/shard_map/unpack/pallas_call | solution.py:459

commit v4 on v3

--- a/solution.py
+++ b/solution.py
@@ -82,6 +82,19 @@
         assert SPAN % self.own == 0 and variables * self.own <= LANES
         assert obs_here % (self.win * LANES) == 0
 
+    def slot(self, d):
+        mem, rest = divmod(d, self.lat * self.win)
+        lat, win = divmod(rest, self.win)
+        return (lat * self.mem + mem) * self.win + win
+
+
+def turn(x):
+    pair = lax.broadcasted_iota(jnp.int32, (ROWS, LANES), 0) // PAIR
+    group = lane_ids() // SPAN
+    x = jnp.where(pair // 2 == group // 2, x, roll(roll(x, LANES // 2, 1), HALF, 0))
+    up, down = roll(roll(x, -PAIR, 0), SPAN, 1), roll(roll(x, PAIR, 0), -SPAN, 1)
+    return jnp.where(pair % 2 == group % 2, x, jnp.where(pair % 2 == 0, up, down))
+
 
 def pack_kernel(z, steps, *refs):
     sources, (out, coup, error), scratch, sems = refs[:9], refs[9:12], refs[12:21], refs[21]
@@ -108,26 +121,28 @@
         for d, part in windows([dif[v] for v in mine], z.own):
             part = jnp.where(spare, count, part)
             for block in range(z.mem):
-                at = (block * per_block + d) * z.chunk + z.dif_at + reg * ROWS
+                at = z.slot(block * per_block + d) * z.chunk + z.dif_at + reg * ROWS
                 out[at : at + ROWS, :] = part
-    copies[3].wait()
+    for copy in copies[3:8]:
+        copy.wait()
+    n = z.obs_rows
+    tables = []
+    for ref in (cell, window, value, weight):
+        rows = ref[0:n, :]
+        for other in range(1, z.win):
+            rows = jnp.where(k == other, ref[other * n : (other + 1) * n, :], rows)
+        tables.append(rows.astype(jnp.float32))
     units = [ens[m, v] for m in range(z.members_here) for v in range(z.vars_here)]
     for reg in range(z.ens_regs):
         for d, part in windows(units[reg * GROUPS : (reg + 1) * GROUPS], z.own):
-            at = d * z.chunk + reg * ROWS
+            at = z.slot(d) * z.chunk + reg * ROWS
             out[at : at + ROWS, :] = part
-    for copy in copies[4:]:
-        copy.wait()
+    copies[8].wait()
     low = lane_ids() < LANES // 2
     for d, part in windows([wts[0, m] for m in range(z.members_here)], z.own):
-        at = d * z.chunk + z.wts_at
+        at = z.slot(d) * z.chunk + z.wts_at
         out[at : at + HALF, :] = jnp.where(low, part, roll(roll(part, LANES // 2, 1), HALF, 0))[:HALF]
-    n = z.obs_rows
-    for a, ref in enumerate((cell, window, value, weight)):
-        rows = ref[0:n, :]
-        for other in range(1, z.win):
-            rows = jnp.where(k == other, ref[other * n : (other + 1) * n, :], rows)
-        rows = rows.astype(jnp.float32)
+    for a, rows in enumerate(tables):
         for d in range(z.devices):
             at = d * z.chunk + z.obs_at + a * n
             out[at : at + n, :] = rows
@@ -143,11 +158,11 @@
 
 
 def place(pieces, width):
-    target = lax.broadcasted_iota(jnp.int32, pieces[0][0].shape, 1) // width
+    block = lane_ids() // width
     out = None
-    for g, (x, lane) in enumerate(pieces):
-        moved = roll(x, width * g - lane, 1)
-        out = moved if out is None else jnp.where(target == g, moved, out)
+    for x, source, target in pieces:
+        moved = roll(x, target - source, 1)
+        out = moved if out is None else jnp.where(block == target // width, moved, out)
     return out
 
 
@@ -173,7 +188,7 @@
         return (mem * z.lat + lat) * z.win + win
 
     def take(mem, lat, win, at, rows):
-        first = source(mem, lat, win) * z.chunk
+        first = ((lat * z.mem + mem) * z.win + win) * z.chunk
         return recv[pl.ds((first if isinstance(first, int) else pl.multiple_of(first, HALF)) + at, rows), :]
 
     for mem in range(z.mem):
@@ -209,7 +224,7 @@
             for t in range(T):
                 quarter = [weights_of(mem, h * T + t, 2 * p + w) for w in range(2) for h in range(2)]
                 for unit in range(z.members_here):
-                    control[mem * z.members_here + unit][p][t] = place([(x, SPAN * unit) for x in quarter], SPAN)
+                    control[mem * z.members_here + unit][p][t] = place([(x, SPAN * unit, SPAN * g) for g, x in enumerate(quarter)], SPAN)
     steps = [jnp.broadcast_to(take(0, 0, win, z.dif_at, 1)[:, :1], (ROWS, LANES)) for win in range(z.win)]
     counts = [jnp.where(group < 2, steps[2 * p], steps[2 * p + 1]).astype(jnp.int32) for p in range(z.pairs)]
 
@@ -370,29 +385,41 @@
         for win in range(z.win):
             p, w = divmod(win, 2)
             lane = SPAN * (2 * w + h) + z.halo
-            grown = place([(increment[p][v][t], lane) for v in range(NV)], z.own)
-            for mem in range(z.mem):
-                to = source(mem, lat, win)
-                mine = [control[mem * z.members_here + m][p][t] for m in range(z.members_here)]
-                x = place([(x, lane) for x in mine], z.own)
-                folded = place([(roll(x, -PAIR * q, 0), 0) for q in range(GROUPS)], SPAN)
-                out[to * z.back : to * z.back + PAIR, :] = folded[:PAIR]
-                out[to * z.back + PAIR : (to + 1) * z.back, :] = grown
+            grown = place([(increment[p][v][t], lane, z.own * v) for v in range(NV)], z.own)
+            for first_mem in range(0, z.mem, GROUPS):
+                mems = range(first_mem, min(z.mem, first_mem + GROUPS))
+                x = place(
+                    [
+                        (control[mem * z.members_here + m][p][t], lane, SPAN * (mem - first_mem) + z.own * m)
+                        for mem in mems
+                        for m in range(z.members_here)
+                    ],
+                    z.own,
+                )
+                x = turn(x)
+                for mem in mems:
+                    to, at = source(mem, lat, win) * z.back, PAIR * (mem - first_mem)
+                    out[to : to + PAIR, :] = x[at : at + PAIR]
+                    out[to + PAIR : to + z.back, :] = grown
 
 
 def unpack_kernel(z, recv, control, increment):
     per_tile = LANES // z.own
     for tile in range(z.lon // LANES):
-        got = [recv[d * z.back : d * z.back + PAIR, :] for d in range(tile * per_tile, (tile + 1) * per_tile)]
+        pieces = []
+        for batch in range(0, per_tile, GROUPS):
+            x = turn(jnp.concatenate(
+                [recv[d * z.back : d * z.back + PAIR, :] for d in range(tile * per_tile + batch, tile * per_tile + batch + GROUPS)], 0
+            ))
+            pieces += [(x, SPAN * g, z.own * (batch + g)) for g in range(GROUPS)]
         for m in range(z.members_here):
-            for q in range(GROUPS):
-                control[0, m, PAIR * q : PAIR * (q + 1), tile * LANES : (tile + 1) * LANES] = place(
-                    [(x, SPAN * q + z.own * m) for x in got], z.own
-                )
+            control[0, m, :, tile * LANES : (tile + 1) * LANES] = place(
+                [(x, source + z.own * m, target) for x, source, target in pieces], z.own
+            )
     first = lax.axis_index("mem") * per_tile
     got = [recv[pl.ds(pl.multiple_of((first + q) * z.back, PAIR) + PAIR, ROWS), :] for q in range(per_tile)]
     for v in range(z.variables):
-        increment[0, v] = place([(x, z.own * v) for x in got], z.own)
+        increment[0, v] = place([(x, z.own * v, z.own * q) for q, x in enumerate(got)], z.own)
 
 
 def in_hbm(*arrays):
@@ -414,10 +441,10 @@
         field = pltpu.VMEM((z.pairs, z.variables, z.tiles, *reg), f32)
         still = pltpu.VMEM((z.variables, z.tiles, *reg), f32)
 
-        def exchange(x, rows):
+        def exchange(x, rows, axes):
             step = math.gcd(rows, ROWS)
             split = x.reshape(z.devices, rows // step, step, LANES)
-            return lax.all_to_all(split, ("mem", "lat", "win"), 0, 0).reshape(x.shape)
+            return lax.all_to_all(split, axes, 0, 0).reshape(x.shape)
 
         sent, coup, error = pl.pallas_call(
             lambda *refs: pack_kernel(z, *refs),
@@ -454,8 +481,8 @@
             ],
             compiler_params=params,
             name="descend",
-        )(coup, error, exchange(sent, z.chunk))
-        home = exchange(back, z.back)
+        )(coup, error, exchange(sent, z.chunk, ("lat", "mem", "win")))
+        home = exchange(back, z.back, ("mem", "lat", "win"))
         return pl.pallas_call(
             lambda *refs: unpack_kernel(z, *refs),
             out_shape=(

time: 49.3 us -> 48.2 us (0.978)
  Pallas kernels: 9.51 us -> 8.56 us
    pallas_call x1, Pallas kernels: 6.67 us -> 5.83 us  [local(): pl.pallas_call(lambda *refs: descend_kernel(z, scale, *refs), out_shape=j...]
where the time goes in v4:
time: 48.2 us; the launch traced here: 48.1 us
  blocking collectives  38.3 us (79%)
  Pallas kernels  8.56 us (18%)
  between operations  1.3 us (3%)
    all_to_all x2, blocking collectives, exchange(): return lax.all_to_all(split, axes, 0, 0).reshape(x.shape)  38.3 us
    pallas_call x1, Pallas kernels, local(): pl.pallas_call(lambda *refs: descend_kernel(z, scale, *refs), out_shape=j...  5.83 us
    pallas_call x1, Pallas kernels, local(): pl.pallas_call(lambda *refs: pack_kernel(z, *refs), out_shape=(jax.ShapeD...  1.86 us

profile of v4, /device:TPU:0, one launch (start us, length us, event | category | flops | bytes accessed | tf_op | source)
XLA Modules:
  0.0 48.1 jit_solution(6995967747884700514)
XLA Ops:
  1.3 1.9 %pack.1 = (f32[1408,128]{1,0:T(8,128)S(1)}, f32[8,8,8,128]{3,2,1,0:T(8,128)S(1)}, f32[8,8,128]{2,1,0:T(8,128)S(1)}) custom-call(s32[1]{0:T(128)S(6)} %copy.12.refs_0_, f32[8,8]{1,0:T(8,128)} %refs_1_.1, f32[1,8]{1,0:T(1,128)} %bitcast.17, f32[8,8,128]{2,1,0:T(8,128)} %refs_3_.1, f32[2,8,8,512]{3,2,1,0:T(8,128)} %refs_4_.1, s32[8,128]{1,0:T(8,128)} %bitcast.13, ...), custom_call_target="tpu_custom_call" | custom-call | tf_op jit(solution)/shard_map/pack/pallas_call | solution.py:449
  3.1 26.3 %all_to_all.10 = f32[32,11,4,128]{3,2,1,0:T(4,128)S(1)} all-to-all(f32[32,11,4,128]{3,2,1,0:T(4,128)S(1)} %bitcast.10), channel_id=1, replica_groups=mesh['mem'=4,'lat'=4,'win'=2] {'lat','mem','win'}, dimensions={0} | all-to-all | bytes 1441792 | tf_op jit(solution)/shard_map/all_to_all | solution.py:447
  29.5 5.8 %descend.1 = f32[320,128]{1,0:T(8,128)S(1)} custom-call(f32[8,8,8,128]{3,2,1,0:T(8,128)S(1)} %get-tuple-element.5.refs_0_, f32[8,8,128]{2,1,0:T(8,128)S(1)} %get-tuple-element.6.refs_1_, f32[1408,128]{1,0:T(8,128)S(1)} %bitcast.9), custom_call_target="tpu_custom_call" | custom-call | tf_op jit(solution)/shard_map/descend/pallas_call | solution.py:470
  35.3 12.0 %all_to_all.11 = f32[32,5,2,128]{3,2,1,0:T(2,128)S(1)} all-to-all(f32[32,5,2,128]{3,2,1,0:T(2,128)S(1)} %bitcast.11), channel_id=1, replica_groups=mesh['mem'=4,'lat'=4,'win'=2] {'mem','lat','win'}, dimensions={0} | all-to-all | bytes 327680 | tf_op jit(solution)/shard_map/all_to_all | solution.py:447
  47.3 0.9 %unpack.1 = (f32[1,2,8,512]{3,2,1,0:T(8,128)}, f32[1,8,8,128]{3,2,1,0:T(8,128)}) custom-call(f32[320,128]{1,0:T(8,128)S(1)} %bitcast.12), custom_call_target="tpu_custom_call" | custom-call | tf_op jit(solution)/shard_map/unpack/pallas_call | solution.py:486

commit v5 on v4

--- a/solution.py
+++ b/solution.py
@@ -229,13 +229,14 @@
     counts = [jnp.where(group < 2, steps[2 * p], steps[2 * p + 1]).astype(jnp.int32) for p in range(z.pairs)]
 
     bf16 = jnp.bfloat16
-    row_id = lax.broadcasted_iota(jnp.int32, (z.win * NV * ROWS, LANES), 0).astype(jnp.float32).astype(bf16)
+    id_type = bf16 if z.win * NV * ROWS <= 256 else jnp.float32
+    row_id = lax.broadcasted_iota(jnp.int32, (z.win * NV * ROWS, LANES), 0).astype(jnp.float32).astype(id_type)
     lane_id = lax.broadcasted_iota(jnp.int32, (SPAN, LANES), 0).astype(jnp.float32).astype(bf16)
     one, none = jnp.ones((), bf16), jnp.zeros((), bf16)
     n = z.obs_rows
 
     def column(x, like):
-        return jnp.broadcast_to(x, like.shape).astype(bf16)
+        return jnp.broadcast_to(x, like.shape).astype(like.dtype)
 
     for lat in range(z.lat):
         hot, parts = [], []
@@ -255,7 +256,7 @@
                 for x in range(n):
                     at = slice(x, x + 1)
                     hit = column(lane[at], lane_id) == lane_id
-                    hot.append(jnp.where(column(row[at], row_id) == row_id, one, none))
+                    hot.append(jnp.where(column(row[at], row_id) == row_id, one.astype(id_type), none.astype(id_type)).astype(bf16))
                     parts.append(jnp.concatenate([jnp.where(hit, column(y[at], lane_id), none) for y in values], 0))
         total = lax.dot_general(
             jnp.concatenate(hot, 1),

time: 48.2 us -> 48.4 us (level)
  no operation moved by 1% of the time
where the time goes in v5:
time: 48.4 us; the launch traced here: 48.5 us
  blocking collectives  38.3 us (79%)
  Pallas kernels  8.93 us (18%)
  between operations  1.3 us (3%)
    all_to_all x2, blocking collectives, exchange(): return lax.all_to_all(split, axes, 0, 0).reshape(x.shape)  38.3 us
    pallas_call x1, Pallas kernels, local(): pl.pallas_call(lambda *refs: descend_kernel(z, scale, *refs), out_shape=j...  6.2 us
    pallas_call x1, Pallas kernels, local(): pl.pallas_call(lambda *refs: pack_kernel(z, *refs), out_shape=(jax.ShapeD...  1.86 us

profile of v5, /device:TPU:0, one launch (start us, length us, event | category | flops | bytes accessed | tf_op | source)
XLA Modules:
  0.0 48.5 jit_solution(6995967747884700514)
XLA Ops:
  1.3 1.9 %pack.1 = (f32[1408,128]{1,0:T(8,128)S(1)}, f32[8,8,8,128]{3,2,1,0:T(8,128)S(1)}, f32[8,8,128]{2,1,0:T(8,128)S(1)}) custom-call(s32[1]{0:T(128)S(6)} %copy.12.refs_0_, f32[8,8]{1,0:T(8,128)} %refs_1_.1, f32[1,8]{1,0:T(1,128)} %bitcast.17, f32[8,8,128]{2,1,0:T(8,128)} %refs_3_.1, f32[2,8,8,512]{3,2,1,0:T(8,128)} %refs_4_.1, s32[8,128]{1,0:T(8,128)} %bitcast.13, ...), custom_call_target="tpu_custom_call" | custom-call | tf_op jit(solution)/shard_map/pack/pallas_call | solution.py:450
  3.1 26.3 %all_to_all.10 = f32[32,11,4,128]{3,2,1,0:T(4,128)S(1)} all-to-all(f32[32,11,4,128]{3,2,1,0:T(4,128)S(1)} %bitcast.10), channel_id=1, replica_groups=mesh['mem'=4,'lat'=4,'win'=2] {'lat','mem','win'}, dimensions={0} | all-to-all | bytes 1441792 | tf_op jit(solution)/shard_map/all_to_all | solution.py:448
  29.5 6.2 %descend.1 = f32[320,128]{1,0:T(8,128)S(1)} custom-call(f32[8,8,8,128]{3,2,1,0:T(8,128)S(1)} %get-tuple-element.5.refs_0_, f32[8,8,128]{2,1,0:T(8,128)S(1)} %get-tuple-element.6.refs_1_, f32[1408,128]{1,0:T(8,128)S(1)} %bitcast.9), custom_call_target="tpu_custom_call" | custom-call | tf_op jit(solution)/shard_map/descend/pallas_call | solution.py:471
  35.7 12.0 %all_to_all.11 = f32[32,5,2,128]{3,2,1,0:T(2,128)S(1)} all-to-all(f32[32,5,2,128]{3,2,1,0:T(2,128)S(1)} %bitcast.11), channel_id=1, replica_groups=mesh['mem'=4,'lat'=4,'win'=2] {'mem','lat','win'}, dimensions={0} | all-to-all | bytes 327680 | tf_op jit(solution)/shard_map/all_to_all | solution.py:448
  47.6 0.9 %unpack.1 = (f32[1,2,8,512]{3,2,1,0:T(8,128)}, f32[1,8,8,128]{3,2,1,0:T(8,128)}) custom-call(f32[320,128]{1,0:T(8,128)S(1)} %bitcast.12), custom_call_target="tpu_custom_call" | custom-call | tf_op jit(solution)/shard_map/unpack/pallas_call | solution.py:487
